TPU v7x, 128 devices: a whole 4x4x4 slice. The times are simulated.
128 devices in a mesh: dp: 32 (over z, x, core), head: 4 (over y).
Axes of the slice: x: 4, y: 4, z: 4, core: 2. Of those that a mesh axis runs over, the one named last changes fastest.
Arguments:
- hidden: bfloat16 [1024, 2048], P('dp'), may hold values from -6 to 6
- attn_gain: float32 [2048], replicated, may hold values from 0.1 to 1.9
- w_query: bfloat16 [2048, 3072], P(None, 'head'), may hold values from -0.125 to 0.125
- w_latent: bfloat16 [2048, 576], P(None, 'head'), may hold values from -0.125 to 0.125
- latent_gain: float32 [512], replicated, may hold values from 0.1 to 1.9
- w_key_up: bfloat16 [16, 128, 512], P('head'), may hold values from -0.5 to 0.5
- w_value_up: bfloat16 [16, 512, 128], P('head'), may hold values from -0.25 to 0.25
- w_out: bfloat16 [2048, 2048], P('head'), may hold values from -0.125 to 0.125
- kv_cache: bfloat16 [1024, 128, 576], P('dp'), may hold values from -110 to 110
- lengths: int32 [1024], P('dp'), may hold values from 1 to 128, 65536 in all
- live_mask: int32 [1024], P('dp'), may hold values 0 or 1
- mlp_gain: float32 [2048], replicated, may hold values from 0.1 to 1.9
- w_router: bfloat16 [2048, 64], replicated, may hold values from -0.125 to 0.125
- routes: int32 [1024, 6], P('dp'), may hold values from 0 to 63, all different within a row; in each aligned block of 32 rows (0 to 31, 32 to 63, ...) at most 6 rows name the same one
- w_experts_in: bfloat16 [64, 2048, 2, 1408], P('dp', None, None, 'head'), may hold values from -0.125 to 0.125
- w_experts_out: bfloat16 [64, 1408, 2048], P('dp', 'head'), may hold values from -0.15625 to 0.15625
- w_shared_in: bfloat16 [2048, 2, 1408], P(None, None, 'head'), may hold values from -0.125 to 0.125
- w_shared_out: bfloat16 [1408, 2048], P('head'), may hold values from -0.15625 to 0.15625
Outputs:
- output: bfloat16 [1024, 2048], P('dp', 'head')
Inputs may be any that keep to these rules, and one draw needn't show every extreme that they name: Among the routes of one device's 32 rows no expert is named more than 6 times, a bound that some block reaches. Request t has cached positions 0 to lengths[t] - 1; some request has 128.
All inputs are finite; a program needn't handle non-finite values. No bound on the sum of `lengths` or of `live_mask` on one device may be relied on, other than what follows from the above.
Results may differ from a plain program's by a relative error of at most 0.02.
The roundings to bfloat16 on the way count: a program that leaves them out, or rounds other values in their place, can miss the bound.
Values may be sent and summed in bfloat16 or wider, within the bound.
A program may use at most 128 MiB of HBM per device.

v0:
```python
import math

import jax
import jax.numpy as jnp
from jax import lax
from jax.sharding import PartitionSpec as P

NOPE = 128
ROPE = 64
VDIM = 128
LAT = 512


norm_eps = 1e-06
rope_theta = 50000.0
route_scale = 2.446


def rms_norm(values, weights):
    mean_square = jnp.mean(values * values, axis=-1, keepdims=True)
    return values * lax.rsqrt(mean_square + norm_eps) * weights


def rotary(values, positions):
    half_size = values.shape[-1] // 2
    frequency = rope_theta ** (-jnp.arange(half_size, dtype=jnp.float32) / half_size)
    angles = positions.reshape((-1,) + (1,) * (values.ndim - 1)) * frequency
    first_half = values[..., :half_size]
    second_half = values[..., half_size:]
    cosine = jnp.cos(angles)
    sine_part = jnp.sin(angles)
    return jnp.concatenate(
        [
            first_half * cosine - second_half * sine_part,
            second_half * cosine + first_half * sine_part,
        ],
        axis=-1,
    )


def body(
    hidden,
    attn_gain,
    w_query,
    w_latent,
    latent_gain,
    w_key_up,
    w_value_up,
    w_out,
    kv_cache,
    lengths,
    live_mask,
    mlp_gain,
    w_router,
    routes,
    w_experts_in,
    w_experts_out,
    w_shared_in,
    w_shared_out,
):
    request_count = hidden.shape[0]
    model_width = hidden.shape[1]
    local_heads = w_key_up.shape[0]
    cache_length = kv_cache.shape[1]
    head_count = lax.axis_size("head")
    share_width = model_width // head_count
    column_start = lax.axis_index("head") * share_width
    dp_count = lax.axis_size("dp")
    local_experts = w_experts_in.shape[0]
    expert_total = local_experts * dp_count
    top_count = routes.shape[1]
    capacity = max(2, 2 * top_count * request_count // expert_total)
    normed = rms_norm(hidden.astype(jnp.float32), attn_gain).astype(jnp.bfloat16)
    query_all = jnp.dot(normed, w_query, preferred_element_type=jnp.float32).reshape(
        request_count, local_heads, NOPE + ROPE
    )
    positions = lengths.astype(jnp.float32)
    query_nope = query_all[..., :NOPE].astype(jnp.bfloat16)
    query_rope = rotary(query_all[..., NOPE:], positions).astype(jnp.bfloat16)
    query_latent = jnp.einsum(
        "rhn,hnc->rhc", query_nope, w_key_up, preferred_element_type=jnp.float32
    ).astype(jnp.bfloat16)
    fresh_part = jnp.dot(normed, w_latent, preferred_element_type=jnp.float32).astype(jnp.bfloat16)
    fresh_kv = lax.all_gather(fresh_part, "head", axis=1, tiled=True)
    latent_new = rms_norm(fresh_kv[:, :LAT].astype(jnp.float32), latent_gain)
    rope_new = rotary(fresh_kv[:, LAT:].astype(jnp.float32), positions)
    key_new = jnp.concatenate([latent_new, rope_new], axis=-1).astype(jnp.bfloat16)
    query_full = jnp.concatenate([query_latent, query_rope], axis=-1)
    inverse_root = 1.0 / math.sqrt(NOPE + ROPE)
    scores = (
        jnp.einsum("rhc,rjc->rhj", query_full, kv_cache, preferred_element_type=jnp.float32)
        * inverse_root
    )
    in_cache = jnp.arange(cache_length, dtype=jnp.int32)[None, :] < lengths[:, None]
    scores = jnp.where(in_cache[:, None, :], scores, -jnp.inf)
    score_new = (
        jnp.einsum("rhc,rc->rh", query_full, key_new, preferred_element_type=jnp.float32)
        * inverse_root
    )
    highest = jnp.maximum(jnp.max(scores, axis=-1), score_new)
    weights_cached = jnp.exp(scores - highest[..., None])
    weight_new = jnp.exp(score_new - highest)
    denominator = jnp.sum(weights_cached, axis=-1) + weight_new
    probabilities = (weights_cached / denominator[..., None]).astype(jnp.bfloat16)
    prob_new = (weight_new / denominator).astype(jnp.bfloat16)
    context = jnp.einsum(
        "rhj,rjc->rhc", probabilities, kv_cache[..., :LAT], preferred_element_type=jnp.float32
    )
    context = (
        context
        + prob_new.astype(jnp.float32)[..., None] * key_new[:, None, :LAT].astype(jnp.float32)
    ).astype(jnp.bfloat16)
    values = jnp.einsum(
        "rhc,hcv->rhv", context, w_value_up, preferred_element_type=jnp.float32
    ).astype(jnp.bfloat16)
    partial_value = jnp.dot(
        values.reshape(request_count, local_heads * VDIM), w_out, preferred_element_type=jnp.float32
    )
    attention = lax.psum(partial_value.astype(jnp.bfloat16), "head").astype(jnp.float32)
    mixed_rows = (hidden.astype(jnp.float32) + attention).astype(jnp.bfloat16)
    ffn_input = rms_norm(mixed_rows.astype(jnp.float32), mlp_gain).astype(jnp.bfloat16)
    mixed_share = lax.dynamic_slice_in_dim(mixed_rows, column_start, share_width, 1)
    logits = jnp.dot(ffn_input, w_router, preferred_element_type=jnp.float32)
    chosen = jax.nn.sigmoid(jnp.take_along_axis(logits, routes, axis=1))
    route_weight = (
        route_scale
        * live_mask.astype(jnp.float32)[:, None]
        * chosen
        / jnp.sum(chosen, axis=1, keepdims=True)
    )
    pair_count = request_count * top_count
    flat_routes = routes.reshape(pair_count)
    live_pairs = jnp.repeat(live_mask, top_count)
    member = (
        (flat_routes[:, None] == jnp.arange(expert_total, dtype=jnp.int32)[None, :])
        & (live_pairs[:, None] == 1)
    ).astype(jnp.int32)
    earlier = jnp.cumsum(member, axis=0) - member
    slot_rank = jnp.sum(earlier * member, axis=1)
    slot_total = expert_total * capacity
    buffer_slot = jnp.where(live_pairs == 1, flat_routes * capacity + slot_rank, slot_total)
    token_of_pair = jnp.arange(pair_count, dtype=jnp.int32) // top_count
    spread = ffn_input[token_of_pair]
    packed = (
        jnp.zeros((slot_total, ffn_input.shape[1]), jnp.bfloat16)
        .at[buffer_slot]
        .set(spread, mode="drop")
    )
    arrived = lax.all_to_all(
        packed.reshape(dp_count, local_experts, capacity, ffn_input.shape[1]),
        "dp",
        split_axis=0,
        concat_axis=0,
        tiled=True,
    )
    gate_up = jnp.einsum(
        "secd,edkf->seckf", arrived, w_experts_in, preferred_element_type=jnp.float32
    )
    acting = (jax.nn.silu(gate_up[..., 0, :]) * gate_up[..., 1, :]).astype(jnp.bfloat16)
    expert_part = jnp.einsum(
        "secf,efd->secd", acting, w_experts_out, preferred_element_type=jnp.float32
    )
    expert_share = lax.psum_scatter(
        expert_part.astype(jnp.bfloat16), "head", scatter_dimension=3, tiled=True
    )
    returned = lax.all_to_all(expert_share, "dp", split_axis=0, concat_axis=0, tiled=True)
    returned_rows = returned.reshape(slot_total, share_width)
    pick_slot = jnp.minimum(buffer_slot, slot_total - 1)
    pair_rows = returned_rows[pick_slot].astype(jnp.float32)
    routed = jnp.sum(
        (route_weight.reshape(pair_count)[:, None] * pair_rows).reshape(
            request_count, top_count, share_width
        ),
        axis=1,
    )
    shared_width = w_shared_out.shape[0]
    shared_pair = jnp.dot(
        ffn_input,
        w_shared_in.reshape(model_width, 2 * shared_width),
        preferred_element_type=jnp.float32,
    ).reshape(request_count, 2, shared_width)
    shared_act = (jax.nn.silu(shared_pair[:, 0]) * shared_pair[:, 1]).astype(jnp.bfloat16)
    shared_part = jnp.dot(shared_act, w_shared_out, preferred_element_type=jnp.float32)
    shared_share = lax.psum_scatter(
        shared_part.astype(jnp.bfloat16), "head", scatter_dimension=1, tiled=True
    ).astype(jnp.float32)
    return (mixed_share.astype(jnp.float32) + shared_share + routed).astype(jnp.bfloat16)


def solution(mesh):
    placed = (
        P("dp", None),
        P(),
        P(None, "head"),
        P(None, "head"),
        P(),
        P("head", None, None),
        P("head", None, None),
        P("head", None),
        P("dp", None, None),
        P("dp"),
        P("dp"),
        P(),
        P(),
        P("dp", None),
        P("dp", None, None, "head"),
        P("dp", "head", None),
        P(None, None, "head"),
        P("head", None),
    )
    return jax.shard_map(
        body, mesh=mesh, in_specs=placed, out_specs=P("dp", "head"), check_vma=False
    )
```

profile of v0, /device:TPU:1, one launch (start us, length us, event | category | flops | bytes accessed | tf_op | source)
XLA Modules:
  0.0 187.7 jit_solution(8351223471823655975)
XLA Ops:
  6.6 0.8 convert_element_type.107
  7.4 0.9 iota_compare_fusion.2
  8.2 1.0 fusion.40
  9.3 1.5 fusion.29
  10.8 10.4 %all-gather = bf16[4,144,32]{1,2,0:T(8,128)(2,1)S(1)} all-gather(bf16[1,144,32]{1,2,0:T(8,128)(2,1)S(1)} %fusion.29), channel_id=1, replica_groups=mesh['dp'=32,'head'=4] {'head'}, dimensions={0}, use_global_device_ids=true | all-gather | bytes 46080 | tf_op jit(solution)/shard_map/all_gather | solution.py:84
  21.2 0.1 reshape.357
  21.3 0.1 fusion.50
  21.5 1.6 fusion.61
  23.0 0.1 reshape.311
  23.2 0.1 fusion.77
  23.3 0.1 fusion.75
  23.4 1.2 fusion.26
  24.7 0.1 subtract_convert_fusion.1
  24.8 0.1 maximum_bitcast_fusion
  24.9 0.1 pad_maximum_fusion
  25.0 0.3 fusion.46
  25.3 3.4 %fusion.78 = (f32[32,4]{1,0:T(8,128)S(1)}, f32[32,4,128]{2,1,0:T(4,128)S(1)}) fusion(bf16[32,128,576]{1,2,0:T(8,128)(2,1)} %param.26, bf16[32,4,576]{2,0,1:T(8,128)(2,1)S(1)} %pad_maximum_fusion, pred[32,128]{1,0:T(8,128)(4,1)S(1)} %iota_compare_fusion.2), kind=kOutput, calls=%fused_computation.128 | convolution fusion | flops 18923392 | bytes 4936192 | tf_op jit(solution)/shard_map/rhc,rjc->rhj/dot_general | solution.py:91
  28.7 0.2 fusion.57
  28.9 0.1 copy-done.1
  29.1 1.2 fusion.23
  30.3 0.2 fusion.28
  30.6 0.3 copy-done.3
  30.8 1.1 convolution_convert_fusion.1
  32.1 0.1 broadcast_in_dim.27
  32.1 0.1 eq.62
  32.2 0.1 eq.57
  32.4 0.1 copy.93
  32.5 0.1 copy.92
  32.6 0.1 mul.265
  32.7 0.1 eq.58
  32.8 0.6 reduce-window.6
  33.4 0.2 slice_reduce_fusion
  33.7 0.1 bitcast_bitcast_fusion
  33.8 41.9 %all-reduce.3.cloned.1.call-done = bf16[32,2048]{1,0:T(8,128)(2,1)} async-done(((bf16[32,2048]{1,0:T(8,128)(2,1)}), bf16[32,2048]{1,0:T(8,128)(2,1)}) %all-reduce.3.cloned.1.call-update) | async-done | bytes 131088 | tf_op jit(solution)/shard_map/psum | solution.py:119
  75.7 1.1 fusion.37
  76.8 0.6 copy-done.5
  77.4 0.1 fusion.39
  77.5 5.6 %scatter_custom_fusion = bf16[384,2048]{1,0:T(8,128)(2,1)} fusion(s32[192]{0:T(256)S(1)} %bitcast.114, bf16[32,2048]{1,0:T(8,128)(2,1)S(1)} %fusion.39, s32[1024]{0:T(1024)S(1)} %pad_clamp_fusion.1, bf16[]{:T(256)} %constant.75.clone.1), kind=kCustom, calls=%fused_computation.28 | custom fusion | bytes 1572866 | tf_op jit(solution)/shard_map/scatter | solution.py:147
  83.1 3.7 %reshape.317 = bf16[32,2,6,2048]{3,2,1,0:T(8,128)(2,1)} reshape(bf16[384,2048]{1,0:T(8,128)(2,1)} %scatter_custom_fusion) | data formatting | bytes 3145728 | tf_op jit(solution)/shard_map/reshape | solution.py:150
  86.8 3.2 %copy.96 = bf16[32,2,6,2048]{3,1,2,0:T(2,128)(2,1)S(1)} copy(bf16[32,2,6,2048]{3,2,1,0:T(8,128)(2,1)} %reshape.317) | data formatting | bytes 3145728 | tf_op jit(solution)/shard_map/reshape | solution.py:150
  90.0 32.3 %all_to_all.10 = bf16[32,2,6,2048]{3,1,2,0:T(2,128)(2,1)S(1)} all-to-all(bf16[32,2,6,2048]{3,1,2,0:T(2,128)(2,1)S(1)} %copy.96), channel_id=1, replica_groups=mesh['dp'=32,'head'=4] {'dp'}, dimensions={0} | all-to-all | bytes 3145728 | tf_op jit(solution)/shard_map/all_to_all | solution.py:149
  122.4 5.9 %fusion.15 = f32[32,2,6,2,352]{4,0,3,2,1:T(8,128)S(1)} fusion(bf16[2,2048,2,352]{1,3,2,0:T(8,128)(2,1)} %param.32, bf16[32,2,6,2048,1]{3,1,2,0,4:T(2,128)(2,1)S(1)} %bitcast.106), kind=kOutput, calls=%fused_computation.17 | convolution fusion | flops 1107296256 | bytes 8421376 | tf_op jit(solution)/shard_map/secd,edkf->seckf/dot_general | solution.py:156
  128.3 2.2 %fusion.11 = bf16[32,2,6,2048]{3,0,2,1:T(8,128)(2,1)} fusion(bf16[2,352,2048]{2,1,0:T(8,128)(2,1)S(1)} %copy-done.10, f32[32,2,6,2,352]{4,0,3,2,1:T(8,128)S(1)} %fusion.15), kind=kOutput, calls=%fused_computation.13 | convolution fusion | flops 555245568 | bytes 5537792 | tf_op jit(solution)/shard_map/secf,efd->secd/dot_general | solution.py:160
  130.5 0.1 copy.89
  130.6 0.1 reshape.337
  130.7 0.6 pad_clamp_fusion
  131.3 1.1 fusion.79
  132.4 1.6 gather_fusion.1
  134.1 0.1 reshape.340
  134.2 0.1 copy.90
  134.3 2.9 %fusion.6 = f32[32,2,352]{2,0,1:T(8,128)S(1)} fusion(bf16[2048,2,352]{0,2,1:T(8,128)(2,1)} %param.34, bf16[32,2048]{1,0:T(8,128)(2,1)S(1)} %fusion.39), kind=kOutput, calls=%fused_computation.10 | convolution fusion | flops 92274688 | bytes 3104768 | tf_op jit(solution)/shard_map/dot_general | solution.py:177
  137.2 1.0 convolution_convert_fusion
  138.3 13.7 %reduce-scatter.5.cloned.1.call-done = bf16[32,2,6,512]{3,0,2,1:T(8,128)(2,1)} async-done(((bf16[32,2,6,2048]{3,0,2,1:T(8,128)(2,1)}), bf16[32,2,6,512]{3,0,2,1:T(8,128)(2,1)}) %reduce-scatter.5.cloned.1.call-update) | async-done | bytes 393232 | tf_op jit(solution)/shard_map/reduce_scatter | solution.py:163
  151.9 2.1 %copy.99 = bf16[32,2,6,512]{3,1,2,0:T(2,128)(2,1)} copy(bf16[32,2,6,512]{3,0,2,1:T(8,128)(2,1)} %reduce-scatter.5.cloned.1.call-done) | data formatting | bytes 786432 | tf_op jit(solution)/shard_map/reduce_scatter | solution.py:163
  154.1 8.6 %all-to-all-start.1 = ((bf16[32,2,6,512]{3,1,2,0:T(2,128)(2,1)}), bf16[32,2,6,512]{3,1,2,0:T(2,128)(2,1)S(1)}, u32[]{:S(2)}, u32[]{:S(2)}) async-start(bf16[32,2,6,512]{3,1,2,0:T(2,128)(2,1)} %copy.99), calls=%async_computation.3 | async-start | bytes 786432 | tf_op jit(solution)/shard_map/all_to_all | solution.py:166
  162.7 0.6 multiply_divide_fusion
  163.3 0.8 copy.91
  164.0 8.8 %all-to-all-done.1 = bf16[32,2,6,512]{3,1,2,0:T(2,128)(2,1)S(1)} async-done(((bf16[32,2,6,512]{3,1,2,0:T(2,128)(2,1)}), bf16[32,2,6,512]{3,1,2,0:T(2,128)(2,1)S(1)}, u32[]{:S(2)}, u32[]{:S(2)}) %all-to-all-start.1) | async-done | bytes 393248 | tf_op jit(solution)/shard_map/all_to_all | solution.py:166
  172.8 0.9 copy.100
  173.7 1.2 reshape.318
  174.9 1.8 gather_fusion
  176.7 1.8 reshape.320
  178.4 1.3 multiply_reduce_fusion
  179.7 1.4 add_convert_fusion
  (51 shorter events, 0.6 us)
Async XLA Ops:
  6.5 14.9 %copy-start = (bf16[2048,768]{1,0:T(8,128)(2,1)S(1)}, bf16[2048,768]{1,0:T(8,128)(2,1)}, u32[]{:S(2)}) copy-start(bf16[2048,768]{1,0:T(8,128)(2,1)} %param.20) | copy-start | bytes 9437188
  6.5 69.2 %all-reduce.3.cloned.1.call-start = ((), (), s32[]{:S(2)}) async-start(), calls=%async_computation.4 | async-start | bytes 262144 | tf_op jit(solution)/shard_map/psum | solution.py:119
  21.2 2.2 %copy-start.9 = (f32[512]{0:T(512)S(1)}, f32[512]{0:T(512)}, u32[]{:S(2)}) copy-start(f32[512]{0:T(512)} %param.22) | copy-start | bytes 6148
  25.3 3.8 %copy-start.1 = (bf16[32,128,576]{1,2,0:T(8,128)(2,1)S(1)}, bf16[32,128,576]{1,2,0:T(8,128)(2,1)}, u32[]{:S(2)}) copy-start(bf16[32,128,576]{1,2,0:T(8,128)(2,1)} %param.26) | copy-start | bytes 14155780
  29.1 1.2 copy-start.6
  29.1 1.8 copy-start.3
  30.3 1.7 copy-start.11
  30.3 2.1 %copy-start.7 = (s32[32,6]{0,1:T(8,128)S(1)}, s32[32,6]{0,1:T(8,128)}, u32[]{:S(2)}) copy-start(s32[32,6]{0,1:T(8,128)} %param.31) | copy-start | bytes 2308
  30.3 45.4 %copy-start.2 = (bf16[32,2048]{1,0:T(8,128)(2,1)S(1)}, bf16[32,2048]{1,0:T(8,128)(2,1)}, u32[]{:S(2)}) copy-start(bf16[32,2048]{1,0:T(8,128)(2,1)} %param.18) | copy-start | bytes 393220
  30.3 47.1 %copy-start.8 = (f32[2048]{0:T(1024)S(1)}, f32[2048]{0:T(1024)}, u32[]{:S(2)}) copy-start(f32[2048]{0:T(1024)} %param.29) | copy-start | bytes 24580
  32.0 120.0 %reduce-scatter.5.cloned.1.call-start = ((), (), s32[]{:S(2)}) async-start(), calls=%async_computation.6 | async-start | bytes 1966080 | tf_op jit(solution)/shard_map/reduce_scatter | solution.py:163
  76.8 0.6 copy-start.5
  122.4 5.9 %copy-start.10 = (bf16[2,352,2048]{2,1,0:T(8,128)(2,1)S(1)}, bf16[2,352,2048]{2,1,0:T(8,128)(2,1)}, u32[]{:S(2)}) copy-start(bf16[2,352,2048]{2,1,0:T(8,128)(2,1)} %param.33) | copy-start | bytes 8650756
  130.4 49.3 %reduce-scatter.3.cloned.1.call-start = ((), (), s32[]{:S(2)}) async-start(), calls=%async_computation.5 | async-start | bytes 163840 | tf_op jit(solution)/shard_map/reduce_scatter | solution.py:184
  134.3 3.0 %copy-start.4 = (bf16[352,2048]{1,0:T(8,128)(2,1)S(1)}, bf16[352,2048]{1,0:T(8,128)(2,1)}, u32[]{:S(2)}) copy-start(bf16[352,2048]{1,0:T(8,128)(2,1)} %param.35) | copy-start | bytes 4325380
  154.1 18.7 %all-to-all-start.1 = ((bf16[32,2,6,512]{3,1,2,0:T(2,128)(2,1)}), bf16[32,2,6,512]{3,1,2,0:T(2,128)(2,1)S(1)}, u32[]{:S(2)}, u32[]{:S(2)}) async-start(bf16[32,2,6,512]{3,1,2,0:T(2,128)(2,1)} %copy.99), calls=%async_computation.3 | async-start | bytes 786432 | tf_op jit(solution)/shard_map/all_to_all | solution.py:166
Sparse Core Ops, SparseCore 0:
  32.1 43.5 all-reduce.2
  130.6 21.3 reduce-scatter.4
  154.4 19.3 reduce-scatter.2
where the time goes:
time: 188 us
  waiting for transfers between devices  64.4 us (34%)
  blocking collectives  42.7 us (23%)
  local copies, waits for them, and re-layouts  25.4 us (14%)
  matrix products  23.6 us (13%)
  between operations  13.4 us (7%)
  other arithmetic  9.43 us (5%)
  starting transfers between devices  8.64 us (5%)
    psum x1, waiting for transfers between devices, body(): lax.psum(partial_value.astype(jnp.bfloat16), 'head').astype(jnp.float32)  41.9 us
    all_to_all x1, blocking collectives, body(): lax.all_to_all(packed.reshape(dp_count, local_experts, capacity, ffn_inpu...  32.3 us
    reduce_scatter x1, waiting for transfers between devices, body(): lax.psum_scatter(expert_part.astype(jnp.bfloat16), 'head', scatter_dimens...  13.7 us
    all_gather x1, blocking collectives, body(): fresh_kv = lax.all_gather(fresh_part, 'head', axis=1, tiled=True)  10.4 us
    all_to_all x1, waiting for transfers between devices, body(): lax.all_to_all(expert_share, 'dp', split_axis=0, concat_axis=0, tiled=True)  8.77 us
    all_to_all x1, starting transfers between devices, body(): lax.all_to_all(expert_share, 'dp', split_axis=0, concat_axis=0, tiled=True)  8.56 us
    reshape x2, local copies, waits for them, and re-layouts, body(): packed.reshape(dp_count, local_experts, capacity, ffn_input.shape[1])  6.93 us
    dot_general x1, matrix products, body(): jnp.einsum('secd,edkf->seckf', arrived, w_experts_in, preferred_element_t...  5.86 us
  transfers between devices with their start and end apart: 4, of which 3 were waited for; matrix products, arithmetic and copies ran while one was open for 11% of the time, Pallas kernels for 0%

commit v1 on v0

v1 whole, which is shorter than its diff:
```python
import functools
import math

import jax
import jax.numpy as jnp
from jax import lax
from jax.experimental import pallas as pl
from jax.experimental.pallas import tpu as pltpu
from jax.sharding import PartitionSpec as P

NOPE = 128
ROPE = 64
VDIM = 128
LAT = 512

norm_eps = 1e-06
rope_theta = 50000.0
route_scale = 2.446

MESH = pl.DeviceIdType.MESH
BF = jnp.bfloat16
F32 = jnp.float32
NT = (((1,), (1,)), ((), ()))
TN = (((0,), (0,)), ((), ()))


def rms_norm(values, weights):
    mean_square = jnp.mean(values * values, axis=-1, keepdims=True)
    return values * lax.rsqrt(mean_square + norm_eps) * weights


def rotary(values, positions):
    half_size = values.shape[-1] // 2
    frequency = rope_theta ** (-jnp.arange(half_size, dtype=jnp.float32) / half_size)
    angles = positions.reshape((-1,) + (1,) * (values.ndim - 1)) * frequency
    first_half = values[..., :half_size]
    second_half = values[..., half_size:]
    cosine = jnp.cos(angles)
    sine_part = jnp.sin(angles)
    return jnp.concatenate(
        [
            first_half * cosine - second_half * sine_part,
            second_half * cosine + first_half * sine_part,
        ],
        axis=-1,
    )


def head_gather_kernel(x_ref, o_ref, ssem, rsem):
    dp, h = lax.axis_index("dp"), lax.axis_index("head")
    barrier = pltpu.get_barrier_semaphore()
    for k in range(1, 4):
        pl.semaphore_signal(barrier, inc=1, device_id=(dp, lax.rem(h + k, 4)), device_id_type=MESH)
    pl.semaphore_wait(barrier, 3)
    copies = []
    for k in range(1, 4):
        copies.append(
            pltpu.make_async_remote_copy(
                src_ref=x_ref,
                dst_ref=o_ref.at[h],
                send_sem=ssem.at[k - 1],
                recv_sem=rsem.at[k - 1],
                device_id=(dp, lax.rem(h + k, 4)),
                device_id_type=MESH,
            )
        )
        copies[-1].start()
    o_ref[h] = x_ref[...]
    for k in range(1, 4):
        pltpu.make_async_remote_copy(
            src_ref=x_ref,
            dst_ref=o_ref.at[lax.rem(h + 4 - k, 4)],
            send_sem=ssem.at[k - 1],
            recv_sem=rsem.at[k - 1],
            device_id=(dp, lax.rem(h + k, 4)),
            device_id_type=MESH,
        ).wait()


def head_gather(x):
    return pl.pallas_call(
        head_gather_kernel,
        out_shape=jax.ShapeDtypeStruct((4,) + x.shape, x.dtype),
        in_specs=[pl.BlockSpec(memory_space=pltpu.VMEM)],
        out_specs=pl.BlockSpec(memory_space=pltpu.VMEM),
        scratch_shapes=[pltpu.SemaphoreType.DMA((3,)), pltpu.SemaphoreType.DMA((3,))],
        compiler_params=pltpu.CompilerParams(collective_id=0, has_side_effects=True),
    )(x)


def moe_kernel(
    part_ref, hid_ref, gain_ref, rt_ref, routes_ref, live_ref, win_hbm, wout_hbm, sin_hbm, sout_hbm,
    out_ref,
    win, wout, sin, sout, yrs, mix, ffn, xb, shared, xs, hid_slot, outs, pmat, wslot, cb, pr, rl, rf, al, af, fin, tot, yr,
    wsem, ssem, rsem,
):
    dp, h = lax.axis_index("dp"), lax.axis_index("head")
    core = lax.rem(dp, 2)
    x = lax.rem(dp // 2, 4)
    z = dp // 8
    a = x + core * (z - x)
    b = z + core * (x - z)
    sa, sb = 2 + 6 * core, 8 - 6 * core
    na, nb = 1 + 3 * core, 4 - 3 * core

    def dev(da, db):
        return (lax.rem(a + da + 4, 4) * sa + lax.rem(b + db + 4, 4) * sb + core, h)

    def num(da, db):
        return lax.rem(a + da + 4, 4) * na + lax.rem(b + db + 4, 4) * nb

    partner = (dp + 1 - 2 * core, h)

    def ypeer(k):
        return (dp, lax.rem(h + k, 4))

    weights = [
        pltpu.make_async_copy(s, d, wsem.at[i])
        for i, (s, d) in enumerate(((sin_hbm, sin), (sout_hbm, sout), (win_hbm, win), (wout_hbm, wout)))
    ]
    for copy in weights:
        copy.start()

    barrier = pltpu.get_barrier_semaphore()
    for peer in (ypeer(1), ypeer(2), ypeer(3), dev(1, 0), dev(-1, 0), dev(0, 1), dev(0, -1), partner):
        pl.semaphore_signal(barrier, inc=1, device_id=peer, device_id_type=MESH)
    pl.semaphore_wait(barrier, 8)

    pending = []

    def send(i, src, dst, peer):
        copy = pltpu.make_async_remote_copy(
            src_ref=src, dst_ref=dst, send_sem=ssem.at[i], recv_sem=rsem.at[i], device_id=peer, device_id_type=MESH
        )
        copy.start()
        pending.append(copy)

    def recv(i, dst):
        pltpu.make_async_remote_copy(
            src_ref=dst, dst_ref=dst, send_sem=ssem.at[i], recv_sem=rsem.at[i], device_id=partner, device_id_type=MESH
        ).wait_recv()

    for k in range(1, 4):
        column = pl.multiple_of(lax.rem(h + k, 4) * 512, 512)
        send(k - 1, part_ref.at[:, pl.ds(column, 512)], yrs.at[k - 1], ypeer(k))
    own = pl.ds(pl.multiple_of(h * 512, 512), 512)
    attention = part_ref[:, own].astype(F32)
    for k in range(1, 4):
        recv(k - 1, yrs.at[k - 1])
        attention = attention + yrs[k - 1].astype(F32)
    mix[h] = (hid_ref[:, own].astype(F32) + attention).astype(BF)
    for k in range(1, 4):
        send(2 + k, mix.at[h], mix.at[h], ypeer(k))
    for k in range(1, 4):
        recv(2 + k, mix.at[lax.rem(h + 4 - k, 4)])
    square = jnp.zeros((32, 1), F32)
    for i in range(4):
        v = mix[i].astype(F32)
        square = square + jnp.sum(v * v, axis=1, keepdims=True)
    scale = lax.rsqrt(square * (1.0 / 2048.0) + norm_eps)
    for i in range(4):
        v = mix[i].astype(F32)
        ffn[:, i * 512 : (i + 1) * 512] = (v * scale * gain_ref[:, i * 512 : (i + 1) * 512]).astype(BF)

    logits = lax.dot_general(rt_ref[...], ffn[...], NT, preferred_element_type=F32)
    expert_id = lax.broadcasted_iota(jnp.int32, (64, 32), 0)
    named = expert_id == routes_ref[0:1, :]
    for k in range(1, 6):
        named = named | (expert_id == routes_ref[k : k + 1, :])
    chosen = jnp.where(named, jax.nn.sigmoid(logits), 0.0)
    weight = route_scale * live_ref[...].astype(F32) * chosen / jnp.sum(chosen, axis=0, keepdims=True)
    w_hi = weight.astype(BF)
    w_lo = (weight - w_hi.astype(F32)).astype(BF)
    eye = (lax.broadcasted_iota(jnp.int32, (32, 32), 0) == lax.broadcasted_iota(jnp.int32, (32, 32), 1)).astype(F32).astype(BF)
    extra = lax.dot_general(eye, jnp.concatenate([w_hi, w_lo], axis=0), NT, preferred_element_type=F32).astype(BF)

    me = num(0, 0)
    rows = pl.ds(pl.multiple_of(me * 64 + core * 32, 32), 32)
    for half in range(2):
        xb[half, rows, 0:1024] = ffn[:, half * 1024 : (half + 1) * 1024]
        xb[half, rows, 1024:1152] = extra

    def block(n, low=0, count=64):
        return xb.at[core, pl.ds(pl.multiple_of(n * 64 + low, 32), count), :]

    def other(n):
        return xb.at[1 - core, pl.ds(pl.multiple_of(n * 64, 32), 64), :]

    G = 8
    PT = G + 20
    send(PT, xb.at[1 - core, rows, :], xb.at[1 - core, rows, :], partner)
    send(PT + 1, xb.at[core, rows, :], xb.at[core, rows, :], partner)
    prow = pl.ds(pl.multiple_of(me * 64 + (1 - core) * 32, 32), 32)
    recv(PT, xb.at[core, prow, :])

    order = (0, -1, 1, 2)

    def spread(j):
        base = G + 4 + 4 * j
        send(base, block(num(order[j], 0)), block(num(order[j], 0)), dev(0, 1))
        send(base + 1, block(num(order[j], 0)), block(num(order[j], 0)), dev(0, -1))

    def to_partner(j, o):
        if (j, o) != (0, 0):
            n = num(order[j], order[o])
            send(PT + 1 + 4 * j + o, block(n), block(n), partner)

    send(G, block(me), block(me), dev(1, 0))
    send(G + 1, block(me), block(me), dev(-1, 0))
    spread(0)

    weights[0].wait()
    weights[1].wait()
    gate = lax.dot_general(ffn[...], sin[0], NT, preferred_element_type=F32)
    up = lax.dot_general(ffn[...], sin[1], NT, preferred_element_type=F32)
    act = (gate / (1.0 + jnp.exp(-gate)) * up).astype(BF)
    for i in range(4):
        shared[i] = jnp.dot(act, sout[:, i * 512 : (i + 1) * 512], preferred_element_type=F32)

    recv(G, block(num(-1, 0)))
    n = num(-1, 0)
    send(G + 2, block(n, 0, 32), block(n, 0, 32), dev(1, 0))
    spread(1)
    recv(G + 1, block(num(1, 0)))
    n = num(1, 0)
    send(G + 3, block(n, 32, 32), block(n, 32, 32), dev(-1, 0))
    spread(2)

    def first(j):
        base = G + 4 + 4 * j
        n = num(order[j], -1)
        recv(base, block(n))
        send(base + 2, block(n, 0, 32), block(n, 0, 32), dev(0, 1))
        n = num(order[j], 1)
        recv(base + 1, block(n))
        send(base + 3, block(n, 32, 32), block(n, 32, 32), dev(0, -1))
        to_partner(j, 1)
        to_partner(j, 2)

    def second(j):
        base = G + 4 + 4 * j
        n = num(order[j], 2)
        recv(base + 2, block(n, 0, 32))
        recv(base + 3, block(n, 32, 32))
        to_partner(j, 3)

    first(0)
    recv(G + 2, block(num(2, 0), 0, 32))
    recv(G + 3, block(num(2, 0), 32, 32))
    spread(3)
    for j in range(1, 4):
        to_partner(j, 0)
    second(0)
    first(1)
    first(2)
    second(1)
    first(3)
    second(2)
    second(3)

    prow2 = pl.ds(pl.multiple_of(me * 64 + (1 - core) * 32, 32), 32)
    recv(PT + 1, xb.at[1 - core, prow2, :])
    for j in range(4):
        for o in range(4):
            if (j, o) != (0, 0):
                recv(PT + 1 + 4 * j + o, other(num(order[o], order[j])))

    lane = lax.broadcasted_iota(jnp.int32, (8, 128), 1)
    row = lax.broadcasted_iota(jnp.int32, (8, 128), 0)
    target = 2 * dp + lax.rem(row, 2) + 64 * (row // 2)
    pick = jnp.where((lane == target) & (row < 4), 1.0, 0.0).astype(BF)
    t_from = lax.broadcasted_iota(jnp.int32, (256, 256), 0)
    t_to = lax.broadcasted_iota(jnp.int32, (256, 256), 1)
    before = jnp.where((t_from < t_to) & (t_from // 32 == t_to // 32), 1.0, 0.0).astype(BF)
    source = lax.broadcasted_iota(jnp.int32, (1, 256), 1) // 32
    slot = lax.broadcasted_iota(jnp.int32, (64, 256), 0)
    for g in range(4):
        info = lax.dot_general(pick, xb[0, g * 256 : (g + 1) * 256, 1024:1152], NT, preferred_element_type=F32)
        mask = jnp.where(info != 0.0, 1.0, 0.0)
        rank = jnp.dot(mask.astype(BF), before, preferred_element_type=F32)
        for e in range(2):
            value = info[e : e + 1, :] + info[2 + e : 3 + e, :]
            place = jnp.where(mask[e : e + 1, :] > 0.0, 8 * source + rank[e : e + 1, :].astype(jnp.int32), -1)
            hit = jnp.where(slot == place, 1.0, 0.0)
            wslot[e, g * 64 : (g + 1) * 64, :] = jnp.broadcast_to(
                jnp.sum(hit * value, axis=1, keepdims=True), (64, 128)
            )
            hit = hit.astype(BF)
            pmat[g, e * 64 : (e + 1) * 64, :] = hit
        for half in range(2):
            got = jnp.dot(
                pmat[g], xb[half, g * 256 : (g + 1) * 256, 0:1024], preferred_element_type=F32
            ).astype(BF)
            for e in range(2):
                xs[e, g * 64 : (g + 1) * 64, half * 1024 : (half + 1) * 1024] = got[e * 64 : (e + 1) * 64]

    weights[2].wait()
    weights[3].wait()
    for e in range(2):
        gate = lax.dot_general(xs[e], win[2 * e], NT, preferred_element_type=F32)
        up = lax.dot_general(xs[e], win[2 * e + 1], NT, preferred_element_type=F32)
        hid_slot[...] = (gate / (1.0 + jnp.exp(-gate)) * up).astype(BF)
        for i in range(4):
            result = jnp.dot(hid_slot[...], wout[e, :, i * 512 : (i + 1) * 512], preferred_element_type=F32)
            result = (result * wslot[e, :, 0:1]).astype(BF)
            for g in range(4):
                outs[g, e * 64 : (e + 1) * 64, i * 512 : (i + 1) * 512] = result[g * 64 : (g + 1) * 64]

    R = PT + 17
    for g in range(4):
        for half in range(2):
            cb[half, g * 256 : (g + 1) * 256, :] = lax.dot_general(
                pmat[g], outs[g, :, half * 1024 : (half + 1) * 1024], TN, preferred_element_type=F32
            ).astype(BF)
        span = pl.ds(g * 256, 256)
        send(R + g, cb.at[1 - core, span, :], pr.at[span, :], partner)
    for g in range(4):
        span = pl.ds(g * 256, 256)
        recv(R + g, pr.at[span, :])
        cb[core, span, :] = (cb[core, span, :].astype(F32) + pr[span, :].astype(F32)).astype(BF)

    def cpart(n, low=0, count=64):
        return pl.ds(pl.multiple_of(n * 64 + low, 32), count)

    def ring(base, here, ahead, behind, far, up_dev, down_dev, lows, fulls, stage):
        if stage == 0:
            send(base, cb.at[core, cpart(far, 0, 32), :], lows.at[0], up_dev)
            send(base + 1, cb.at[core, cpart(far, 32, 32), :], lows.at[1], down_dev)
        elif stage == 1:
            recv(base, lows.at[0])
            s = cpart(ahead, 0, 32)
            cb[core, s, :] = (cb[core, s, :].astype(F32) + lows[0].astype(F32)).astype(BF)
            send(base + 2, cb.at[core, cpart(ahead), :], fulls.at[0], up_dev)
            recv(base + 1, lows.at[1])
            s = cpart(behind, 32, 32)
            cb[core, s, :] = (cb[core, s, :].astype(F32) + lows[1].astype(F32)).astype(BF)
            send(base + 3, cb.at[core, cpart(behind), :], fulls.at[1], down_dev)
        else:
            recv(base + 2, fulls.at[0])
            recv(base + 3, fulls.at[1])
            s = cpart(here)
            cb[core, s, :] = (cb[core, s, :].astype(F32) + fulls[0].astype(F32) + fulls[1].astype(F32)).astype(BF)

    S = R + 4
    back = (2, 1, -1, 0)

    def bring(j, stage):
        d = back[j]
        ring(S + 4 * j, num(d, 0), num(d, 1), num(d, -1), num(d, 2), dev(0, 1), dev(0, -1), rl.at[j], rf.at[j], stage)

    def aring(stage):
        ring(S + 16, num(0, 0), num(1, 0), num(-1, 0), num(2, 0), dev(1, 0), dev(-1, 0), al, af, stage)

    for j in range(4):
        bring(j, 0)
    for j in range(4):
        bring(j, 1)
    bring(0, 2)
    aring(0)
    bring(1, 2)
    bring(2, 2)
    aring(1)
    bring(3, 2)
    aring(2)

    F = S + 20
    send(F, cb.at[core, prow, :], fin, partner)
    for i in range(2):
        tot[2 * core + i] = (shared[2 * core + i] + cb[core, rows, i * 512 : (i + 1) * 512].astype(F32)).astype(BF)
    recv(F, fin)
    for i in range(2):
        tot[2 * (1 - core) + i] = (shared[2 * (1 - core) + i] + fin[:, i * 512 : (i + 1) * 512].astype(F32)).astype(BF)
    for k in range(1, 4):
        send(F + k, tot.at[lax.rem(h + k, 4)], yr.at[k - 1], ypeer(k))
    result = mix[h].astype(F32) + tot[h].astype(F32)
    for k in range(1, 4):
        recv(F + k, yr.at[k - 1])
        result = result + yr[k - 1].astype(F32)
    out_ref[...] = result.astype(BF)
    for copy in pending:
        copy.wait_send()


MESSAGES = 8 + 20 + 17 + 4 + 20 + 4


def moe(part, hidden, gain, router_t, routes_t, live, win, wout, sin, sout):
    vmem = pl.BlockSpec(memory_space=pltpu.VMEM)
    hbm = pl.BlockSpec(memory_space=pl.ANY)
    return pl.pallas_call(
        moe_kernel,
        out_shape=jax.ShapeDtypeStruct((32, 512), BF),
        in_specs=[vmem] * 6 + [hbm] * 4,
        out_specs=vmem,
        scratch_shapes=[
            pltpu.VMEM((4, 352, 2048), BF),
            pltpu.VMEM((2, 352, 2048), BF),
            pltpu.VMEM((2, 352, 2048), BF),
            pltpu.VMEM((352, 2048), BF),
            pltpu.VMEM((3, 32, 512), BF),
            pltpu.VMEM((4, 32, 512), BF),
            pltpu.VMEM((32, 2048), BF),
            pltpu.VMEM((2, 1024, 1152), BF),
            pltpu.VMEM((4, 32, 512), F32),
            pltpu.VMEM((2, 256, 2048), BF),
            pltpu.VMEM((256, 352), BF),
            pltpu.VMEM((4, 128, 2048), BF),
            pltpu.VMEM((4, 128, 256), BF),
            pltpu.VMEM((2, 256, 128), F32),
            pltpu.VMEM((2, 1024, 1024), BF),
            pltpu.VMEM((1024, 1024), BF),
            pltpu.VMEM((4, 2, 32, 1024), BF),
            pltpu.VMEM((4, 2, 64, 1024), BF),
            pltpu.VMEM((2, 32, 1024), BF),
            pltpu.VMEM((2, 64, 1024), BF),
            pltpu.VMEM((32, 1024), BF),
            pltpu.VMEM((4, 32, 512), BF),
            pltpu.VMEM((3, 32, 512), BF),
            pltpu.SemaphoreType.DMA((4,)),
            pltpu.SemaphoreType.DMA((MESSAGES,)),
            pltpu.SemaphoreType.DMA((MESSAGES,)),
        ],
        compiler_params=pltpu.CompilerParams(collective_id=1, has_side_effects=True, vmem_limit_bytes=60 << 20),
    )(part, hidden, gain, router_t, routes_t, live, win, wout, sin, sout)


def body(
    hidden,
    attn_gain,
    w_query,
    w_latent,
    latent_gain,
    w_key_up,
    w_value_up,
    w_out,
    kv_cache,
    lengths,
    live_mask,
    mlp_gain,
    w_router,
    routes,
    w_experts_in,
    w_experts_out,
    w_shared_in,
    w_shared_out,
):
    request_count = hidden.shape[0]
    local_heads = w_key_up.shape[0]
    cache_length = kv_cache.shape[1]
    normed = rms_norm(hidden.astype(jnp.float32), attn_gain).astype(jnp.bfloat16)
    query_all = jnp.dot(normed, w_query, preferred_element_type=jnp.float32).reshape(
        request_count, local_heads, NOPE + ROPE
    )
    positions = lengths.astype(jnp.float32)
    query_nope = query_all[..., :NOPE].astype(jnp.bfloat16)
    query_rope = rotary(query_all[..., NOPE:], positions).astype(jnp.bfloat16)
    query_latent = jnp.einsum(
        "rhn,hnc->rhc", query_nope, w_key_up, preferred_element_type=jnp.float32
    ).astype(jnp.bfloat16)
    fresh_part = jnp.dot(normed, w_latent, preferred_element_type=jnp.float32).astype(jnp.bfloat16)
    width = fresh_part.shape[1]
    gathered = head_gather(jnp.pad(fresh_part, ((0, 0), (0, 256 - width))))
    fresh_kv = jnp.concatenate([gathered[i, :, :width] for i in range(4)], axis=1)
    latent_new = rms_norm(fresh_kv[:, :LAT].astype(jnp.float32), latent_gain)
    rope_new = rotary(fresh_kv[:, LAT:].astype(jnp.float32), positions)
    key_new = jnp.concatenate([latent_new, rope_new], axis=-1).astype(jnp.bfloat16)
    query_full = jnp.concatenate([query_latent, query_rope], axis=-1)
    inverse_root = 1.0 / math.sqrt(NOPE + ROPE)
    scores = (
        jnp.einsum("rhc,rjc->rhj", query_full, kv_cache, preferred_element_type=jnp.float32)
        * inverse_root
    )
    in_cache = jnp.arange(cache_length, dtype=jnp.int32)[None, :] < lengths[:, None]
    scores = jnp.where(in_cache[:, None, :], scores, -jnp.inf)
    score_new = (
        jnp.einsum("rhc,rc->rh", query_full, key_new, preferred_element_type=jnp.float32)
        * inverse_root
    )
    highest = jnp.maximum(jnp.max(scores, axis=-1), score_new)
    weights_cached = jnp.exp(scores - highest[..., None])
    weight_new = jnp.exp(score_new - highest)
    denominator = jnp.sum(weights_cached, axis=-1) + weight_new
    probabilities = (weights_cached / denominator[..., None]).astype(jnp.bfloat16)
    prob_new = (weight_new / denominator).astype(jnp.bfloat16)
    context = jnp.einsum(
        "rhj,rjc->rhc", probabilities, kv_cache[..., :LAT], preferred_element_type=jnp.float32
    )
    context = (
        context
        + prob_new.astype(jnp.float32)[..., None] * key_new[:, None, :LAT].astype(jnp.float32)
    ).astype(jnp.bfloat16)
    values = jnp.einsum(
        "rhc,hcv->rhv", context, w_value_up, preferred_element_type=jnp.float32
    ).astype(jnp.bfloat16)
    partial_value = jnp.dot(
        values.reshape(request_count, local_heads * VDIM), w_out, preferred_element_type=jnp.float32
    ).astype(jnp.bfloat16)
    experts_in = jnp.transpose(w_experts_in, (0, 2, 3, 1)).reshape(4, 352, 2048)
    shared_in = jnp.transpose(w_shared_in, (1, 2, 0))
    return moe(
        partial_value,
        hidden,
        mlp_gain.reshape(1, -1),
        w_router.T,
        routes.T,
        live_mask.reshape(1, -1),
        experts_in,
        w_experts_out,
        shared_in,
        w_shared_out,
    )


def solution(mesh):
    placed = (
        P("dp", None),
        P(),
        P(None, "head"),
        P(None, "head"),
        P(),
        P("head", None, None),
        P("head", None, None),
        P("head", None),
        P("dp", None, None),
        P("dp"),
        P("dp"),
        P(),
        P(),
        P("dp", None),
        P("dp", None, None, "head"),
        P("dp", "head", None),
        P(None, None, "head"),
        P("head", None),
    )
    return jax.shard_map(
        body, mesh=mesh, in_specs=placed, out_specs=P("dp", "head"), check_vma=False
    )
```

time: 188 us -> 97.7 us (0.52)
  Pallas kernels: 0 us -> 77.9 us
  waiting for transfers between devices: 64.4 us -> 0 us
  blocking collectives: 42.7 us -> 0 us
  local copies, waits for them, and re-layouts: 25.4 us -> 3.87 us
  between operations: 13.4 us -> 0.18 us
  matrix products: 23.6 us -> 13.1 us
  starting transfers between devices: 8.64 us -> 0 us
  other arithmetic: 9.43 us -> 2.22 us
    pallas_call x0 -> x2, Pallas kernels: none -> 77.9 us  [the longest x1 70.5 us: moe(): pl.pallas_call(moe_kernel, out_shape=jax.ShapeDtypeStruct((32, 512), BF),...]
    psum x1 -> x0, waiting for transfers between devices: 41.9 us -> none  [body(): lax.psum(partial_value.astype(jnp.bfloat16), 'head').astype(jnp.float32)]
    all_to_all x1 -> x0, blocking collectives: 32.3 us -> none  [body(): lax.all_to_all(packed.reshape(dp_count, local_experts, capacity, ffn_inpu...]
    reduce_scatter x2 -> x0, waiting for transfers between devices: 13.7 us -> none  [the longest x1 13.7 us: body(): lax.psum_scatter(expert_part.astype(jnp.bfloat16), 'head', scatter_dimens...]
    dot_general x5 -> x0, matrix products: 13.1 us -> none  [the longest x1 5.86 us: body(): jnp.einsum('secd,edkf->seckf', arrived, w_experts_in, preferred_element_t...]
    all_gather x1 -> x0, blocking collectives: 10.4 us -> none  [body(): fresh_kv = lax.all_gather(fresh_part, 'head', axis=1, tiled=True)]
    all_to_all x1 -> x0, waiting for transfers between devices: 8.77 us -> none  [body(): lax.all_to_all(expert_share, 'dp', split_axis=0, concat_axis=0, tiled=True)]
    all_to_all x1 -> x0, starting transfers between devices: 8.56 us -> none  [body(): lax.all_to_all(expert_share, 'dp', split_axis=0, concat_axis=0, tiled=True)]
  transfers between devices with their start and end apart: 4 -> 0, of which waited for: 3 -> 0; matrix products, arithmetic and copies ran while one was open for 11% -> 0% of each run, Pallas kernels for 0% -> 0%
where the time goes in v1:
time: 97.7 us; the launch traced here: 97.3 us
  Pallas kernels  77.9 us (80%)
  matrix products  13.1 us (13%)
  local copies, waits for them, and re-layouts  3.87 us (4%)
  other arithmetic  2.22 us (2%)
    pallas_call x1, Pallas kernels, moe(): pl.pallas_call(moe_kernel, out_shape=jax.ShapeDtypeStruct((32, 512), BF),...  70.5 us
    pallas_call x1, Pallas kernels, head_gather(): pl.pallas_call(head_gather_kernel, out_shape=jax.ShapeDtypeStruct((4,) +...  7.43 us
    dot_general x1, matrix products, body(): jnp.einsum('rhc,rjc->rhj', query_full, kv_cache, preferred_element_type=j...  3.37 us
    dot_general x1, matrix products, body(): jnp.dot(values.reshape(request_count, local_heads * VDIM), w_out, preferr...  2.7 us
    unnamed x13, local copies, waits for them, and re-layouts  2.13 us

profile of v1, /device:TPU:1, one launch (start us, length us, event | category | flops | bytes accessed | tf_op | source)
XLA Modules:
  0.0 97.3 jit_solution(5277736543609885097)
XLA Ops:
  0.0 0.0 copy-start
  0.0 0.0 copy-start.2
  0.0 0.0 copy-start.3
  0.0 0.0 copy-start.5
  0.0 1.2 %fusion.5 = f32[32]{0:T(128)S(1)} fusion(bf16[32,2048]{1,0:T(8,128)(2,1)} %hid_ref.1), kind=kLoop, calls=%fused_computation.12 | loop fusion | flops 196576 | bytes 131200 | tf_op jit(solution)/shard_map/reduce_sum | solution.py:28
  1.2 0.7 copy-done
  2.0 1.6 %fusion.21 = f32[32,768]{1,0:T(8,128)S(1)} fusion(bf16[2048,768]{1,0:T(8,128)(2,1)S(1)} %copy-done, bf16[32,2048]{1,0:T(8,128)(2,1)} %hid_ref.1, f32[2048]{0:T(1024)} %param.19, f32[32]{0:T(128)S(1)} %add_rsqrt_fusion.1), kind=kOutput, calls=%fused_computation.36 | convolution fusion | flops 100925440 | bytes 3383424 | tf_op jit(solution)/shard_map/dot_general | solution.py:451
  3.5 0.1 reshape.124
  3.7 0.1 fusion.31
  3.8 0.0 copy-done.2
  3.8 0.0 copy-done.3
  3.8 1.4 %convolution_convert_fusion.3 = bf16[32,144]{1,0:T(8,128)(2,1)S(1)} fusion(bf16[2048,144]{0,1:T(8,128)(2,1)} %param.21, bf16[32,2048]{1,0:T(8,128)(2,1)S(1)} %copy-done.2, f32[2048]{0:T(1024)S(1)} %copy-done.3, f32[32]{0:T(128)S(1)} %add_rsqrt_fusion.1), kind=kOutput, calls=%fused_computation.9 | convolution fusion | flops 19141120 | bytes 738432 | tf_op jit(solution)/shard_map/dot_general | solution.py:460
  5.2 0.6 pad.4.x_ref
  5.8 7.4 %shard_map.172 = bf16[4,32,256]{2,1,0:T(8,128)(2,1)} custom-call(bf16[32,256]{1,0:T(8,128)(2,1)} %pad.4.x_ref), custom_call_target="tpu_custom_call" | custom-call | tf_op jit(solution)/shard_map/pallas_call | solution.py:81
  13.3 0.8 slice_bitcast_fusion.3
  14.0 0.1 slice_convert_fusion
  14.1 0.0 copy-done.5
  14.2 0.1 subtract_convert_fusion.1
  14.3 0.0 copy-start.4
  14.4 1.2 %fusion.2 = bf16[32,4,512]{2,0,1:T(8,128)(2,1)S(1)} fusion(bf16[4,128,512]{2,1,0:T(8,128)(2,1)} %param.23, bf16[32,4,128]{2,1,0:T(4,128)(2,1)S(1)} %slice.56), kind=kOutput, calls=%fused_computation.4 | convolution fusion | flops 16842752 | bytes 688128 | tf_op jit(solution)/shard_map/rhn,hnc->rhc/dot_general | solution.py:457
  15.6 0.1 pad_maximum_fusion
  15.7 0.1 iota_compare_fusion
  15.8 0.0 copy-start.1
  15.8 3.4 %fusion.32 = (f32[32,4]{1,0:T(8,128)S(1)}, f32[32,4,128]{2,1,0:T(4,128)S(1)}) fusion(bf16[32,128,576]{1,2,0:T(8,128)(2,1)} %param.26, bf16[32,4,576]{2,0,1:T(8,128)(2,1)S(1)} %pad_maximum_fusion, pred[32,128]{1,0:T(8,128)(4,1)S(1)} %iota_compare_fusion), kind=kOutput, calls=%fused_computation.64 | convolution fusion | flops 18923392 | bytes 4936192 | tf_op jit(solution)/shard_map/rhc,rjc->rhj/dot_general | solution.py:470
  19.1 0.2 fusion.16
  19.4 0.0 copy-done.4
  19.4 0.1 fusion.29
  19.5 0.1 maximum_bitcast_fusion
  19.6 0.3 fusion.12
  19.8 0.2 fusion.19
  20.1 0.0 copy-done.1
  20.1 1.2 %fusion = f32[32,4,512]{2,1,0:T(4,128)S(1)} fusion(bf16[32,128,576]{1,2,0:T(8,128)(2,1)S(1)} %copy-done.1, f32[32,4,128]{2,1,0:T(4,128)S(1)} %get-tuple-element.22, f32[32,4]{1,0:T(8,128)S(1)} %get-tuple-element.16, f32[32,4]{1,0:T(8,128)S(1)} %multiply_maximum_fusion), kind=kOutput, calls=%fused_computation | convolution fusion | flops 16826368 | bytes 4554752 | tf_op jit(solution)/shard_map/rhj,rjc->rhc/dot_general | solution.py:485
  21.3 0.1 copy.28
  21.4 1.3 %fusion.4 = bf16[4,4,8,128]{3,2,1,0:T(8,128)(2,1)S(1)} fusion(bf16[4,512,128]{2,1,0:T(8,128)(2,1)} %param.24, f32[32,4,512]{2,1,0:T(4,128)S(1)} %fusion, f32[32,512]{1,0:T(8,128)S(1)} %get-tuple-element.5, f32[32,4]{0,1:T(4,128)S(1)} %copy.28), kind=kOutput, calls=%fused_computation.8 | convolution fusion | flops 16990208 | bytes 885248 | tf_op jit(solution)/shard_map/rhc,hcv->rhv/dot_general | solution.py:492
  22.7 2.7 %convolution_convert_fusion.part_ref = bf16[32,2048]{1,0:T(8,128)(2,1)} fusion(bf16[512,2048]{1,0:T(8,128)(2,1)} %param.25, bf16[4,4,8,128]{3,2,1,0:T(8,128)(2,1)S(1)} %fusion.4), kind=kOutput, calls=%fused_computation.2 | convolution fusion | flops 67174400 | bytes 2260992 | tf_op jit(solution)/shard_map/dot_general | solution.py:495
  25.4 70.5 %shard_map.173 = bf16[32,512]{1,0:T(8,128)(2,1)} custom-call(bf16[32,2048]{1,0:T(8,128)(2,1)} %convolution_convert_fusion.part_ref, bf16[32,2048]{1,0:T(8,128)(2,1)} %hid_ref.1, f32[1,2048]{1,0:T(1,128)} %bitcast.39, bf16[64,2048]{1,0:T(8,128)(2,1)} %bitcast.36, s32[6,32]{1,0:T(8,128)} %bitcast.40, s32[1,32]{1,0:T(1,128)} %bitcast.41, ...), custom_call_target="tpu_custom_call" | custom-call | tf_op jit(solution)/shard_map/pallas_call | solution.py:390
  95.9 1.4 %copy.60 = bf16[32,512]{1,0:T(8,128)(2,1)} copy(bf16[32,512]{1,0:T(8,128)(2,1)} %shard_map.173) | data formatting | bytes 65536
  (8 shorter events, 0.1 us)
Async XLA Ops:
  0.0 2.0 %copy-start = (bf16[2048,768]{1,0:T(8,128)(2,1)S(1)}, bf16[2048,768]{1,0:T(8,128)(2,1)}, u32[]{:S(2)}) copy-start(bf16[2048,768]{1,0:T(8,128)(2,1)} %param.20) | copy-start | bytes 9437188
  0.0 3.8 %copy-start.2 = (bf16[32,2048]{1,0:T(8,128)(2,1)S(1)}, bf16[32,2048]{1,0:T(8,128)(2,1)}, u32[]{:S(2)}) copy-start(bf16[32,2048]{1,0:T(8,128)(2,1)} %hid_ref.1) | copy-start | bytes 393220
  0.0 3.8 %copy-start.3 = (f32[2048]{0:T(1024)S(1)}, f32[2048]{0:T(1024)}, u32[]{:S(2)}) copy-start(f32[2048]{0:T(1024)} %param.19) | copy-start | bytes 24580
  0.0 14.1 %copy-start.5 = (s32[32]{0:T(128)S(1)}, s32[32]{0:T(128)}, u32[]{:S(2)}) copy-start(s32[32]{0:T(128)} %param.27) | copy-start | bytes 388
  14.3 5.1 %copy-start.4 = (f32[512]{0:T(512)S(1)}, f32[512]{0:T(512)}, u32[]{:S(2)}) copy-start(f32[512]{0:T(512)} %param.22) | copy-start | bytes 6148
  15.8 4.3 %copy-start.1 = (bf16[32,128,576]{1,2,0:T(8,128)(2,1)S(1)}, bf16[32,128,576]{1,2,0:T(8,128)(2,1)}, u32[]{:S(2)}) copy-start(bf16[32,128,576]{1,2,0:T(8,128)(2,1)} %param.26) | copy-start | bytes 14155780

commit v2 on v1

--- a/solution.py
+++ b/solution.py
@@ -89,10 +89,11 @@
 
 
 def moe_kernel(
-    part_ref, hid_ref, gain_ref, rt_ref, routes_ref, live_ref, win_hbm, wout_hbm, sin_hbm, sout_hbm,
+    ctx_ref, hid_ref, gain_ref, rt_ref, routes_ref, live_ref, wvu_hbm, wo_hbm, win_hbm, wout_hbm, sin_hbm, sout_hbm,
     out_ref,
-    win, wout, sin, sout, yrs, mix, ffn, xb, shared, xs, hid_slot, outs, pmat, wslot, cb, pr, rl, rf, al, af, fin, tot, yr,
-    wsem, ssem, rsem,
+    wvu, wo, part, win, wout, sin, sout, yrs, mix, ffn, xb, shared, gate_s, xs, hid_slot, outs, pmat, wslot, cb, pr, rl, rf,
+    al, af, fr, yr,
+    wsem, ssem, rsem, fsem,
 ):
     dp, h = lax.axis_index("dp"), lax.axis_index("head")
     core = lax.rem(dp, 2)
@@ -116,15 +117,32 @@
 
     weights = [
         pltpu.make_async_copy(s, d, wsem.at[i])
-        for i, (s, d) in enumerate(((sin_hbm, sin), (sout_hbm, sout), (win_hbm, win), (wout_hbm, wout)))
+        for i, (s, d) in enumerate(
+            (
+                (sin_hbm, sin),
+                (sout_hbm, sout),
+                (win_hbm, win),
+                (wout_hbm, wout),
+            )
+        )
     ]
-    for copy in weights:
+    first_weights = [pltpu.make_async_copy(wvu_hbm, wvu, wsem.at[4]), pltpu.make_async_copy(wo_hbm, wo, wsem.at[5])]
+    for copy in first_weights + weights:
         copy.start()
 
     barrier = pltpu.get_barrier_semaphore()
-    for peer in (ypeer(1), ypeer(2), ypeer(3), dev(1, 0), dev(-1, 0), dev(0, 1), dev(0, -1), partner):
+    other_dp = dp + 1 - 2 * core
+    diagonal = tuple((other_dp, lax.rem(h + k, 4)) for k in range(1, 4))
+    for peer in (ypeer(1), ypeer(2), ypeer(3), dev(1, 0), dev(-1, 0), dev(0, 1), dev(0, -1), partner) + diagonal:
         pl.semaphore_signal(barrier, inc=1, device_id=peer, device_id_type=MESH)
-    pl.semaphore_wait(barrier, 8)
+    first_weights[0].wait()
+    values = jnp.concatenate(
+        [jnp.dot(ctx_ref[i], wvu[i], preferred_element_type=F32).astype(BF) for i in range(4)], axis=1
+    )
+    first_weights[1].wait()
+    for i in range(4):
+        part[i] = jnp.dot(values, wo[:, i * 512 : (i + 1) * 512], preferred_element_type=F32).astype(BF)
+    pl.semaphore_wait(barrier, 11)
 
     pending = []
 
@@ -141,10 +159,9 @@
         ).wait_recv()
 
     for k in range(1, 4):
-        column = pl.multiple_of(lax.rem(h + k, 4) * 512, 512)
-        send(k - 1, part_ref.at[:, pl.ds(column, 512)], yrs.at[k - 1], ypeer(k))
+        send(k - 1, part.at[lax.rem(h + k, 4)], yrs.at[k - 1], ypeer(k))
     own = pl.ds(pl.multiple_of(h * 512, 512), 512)
-    attention = part_ref[:, own].astype(F32)
+    attention = part[h].astype(F32)
     for k in range(1, 4):
         recv(k - 1, yrs.at[k - 1])
         attention = attention + yrs[k - 1].astype(F32)
@@ -211,12 +228,21 @@
 
     weights[0].wait()
     weights[1].wait()
-    gate = lax.dot_general(ffn[...], sin[0], NT, preferred_element_type=F32)
-    up = lax.dot_general(ffn[...], sin[1], NT, preferred_element_type=F32)
-    act = (gate / (1.0 + jnp.exp(-gate)) * up).astype(BF)
-    for i in range(4):
-        shared[i] = jnp.dot(act, sout[:, i * 512 : (i + 1) * 512], preferred_element_type=F32)
-
+
+    def shared_gate():
+        gate_s[...] = lax.dot_general(ffn[...], sin[0], NT, preferred_element_type=F32)
+
+    def shared_up():
+        gate = gate_s[...]
+        up = lax.dot_general(ffn[...], sin[1], NT, preferred_element_type=F32)
+        hid_slot[0:32, :] = (gate / (1.0 + jnp.exp(-gate)) * up).astype(BF)
+
+    def shared_down(i):
+        shared[i] = jnp.dot(
+            hid_slot[0:32, :], sout[:, i * 512 : (i + 1) * 512], preferred_element_type=F32
+        ).astype(BF)
+
+    shared_gate()
     recv(G, block(num(-1, 0)))
     n = num(-1, 0)
     send(G + 2, block(n, 0, 32), block(n, 0, 32), dev(1, 0))
@@ -225,6 +251,7 @@
     n = num(1, 0)
     send(G + 3, block(n, 32, 32), block(n, 32, 32), dev(-1, 0))
     spread(2)
+    shared_up()
 
     def first(j):
         base = G + 4 + 4 * j
@@ -250,11 +277,18 @@
     spread(3)
     for j in range(1, 4):
         to_partner(j, 0)
+    shared_down(0)
+    first(1)
+    shared_down(1)
+    first(2)
+    shared_down(2)
     second(0)
-    first(1)
-    first(2)
+    shared_down(3)
+    first(3)
+    F = PT + 17 + 4 + 20
+    for k in range(1, 4):
+        send(F + k, shared.at[lax.rem(h + k, 4)], yr.at[k - 1], ypeer(k))
     second(1)
-    first(3)
     second(2)
     second(3)
 
@@ -363,36 +397,75 @@
     bring(3, 2)
     aring(2)
 
-    F = S + 20
-    send(F, cb.at[core, prow, :], fin, partner)
-    for i in range(2):
-        tot[2 * core + i] = (shared[2 * core + i] + cb[core, rows, i * 512 : (i + 1) * 512].astype(F32)).astype(BF)
-    recv(F, fin)
-    for i in range(2):
-        tot[2 * (1 - core) + i] = (shared[2 * (1 - core) + i] + fin[:, i * 512 : (i + 1) * 512].astype(F32)).astype(BF)
-    for k in range(1, 4):
-        send(F + k, tot.at[lax.rem(h + k, 4)], yr.at[k - 1], ypeer(k))
-    result = mix[h].astype(F32) + tot[h].astype(F32)
+    local = []
+    for q in range(2):
+        owner = 2 * core + q
+        for t, (span, where) in enumerate(((rows, dp), (prow, other_dp))):
+            copy = pltpu.make_async_remote_copy(
+                src_ref=cb.at[core, span, pl.ds(q * 512, 512)],
+                dst_ref=fr.at[h],
+                send_sem=fsem.at[2 * q + t],
+                recv_sem=fsem.at[4 + h],
+                device_id=(where, owner),
+                device_id_type=MESH,
+            )
+            if t == 1:
+                copy.start()
+                pending.append(copy)
+            else:
+                pl.when(owner != h)(copy.start)
+                local.append((owner, copy))
+    result = mix[h].astype(F32) + shared[h].astype(F32)
     for k in range(1, 4):
         recv(F + k, yr.at[k - 1])
         result = result + yr[k - 1].astype(F32)
+
+    def routed_recv(o):
+        pltpu.make_async_remote_copy(
+            src_ref=fr.at[o],
+            dst_ref=fr.at[o],
+            send_sem=fsem.at[0],
+            recv_sem=fsem.at[4 + o],
+            device_id=partner,
+            device_id_type=MESH,
+        ).wait_recv()
+
+    mine = core == h // 2
+
+    @pl.when(mine)
+    def _():
+        fr[h] = cb[core, rows, pl.ds(pl.multiple_of(lax.rem(h, 2) * 512, 512), 512)]
+
+    @pl.when(jnp.logical_not(mine))
+    def _():
+        routed_recv(h)
+
+    for k in range(1, 4):
+        routed_recv(lax.rem(h + k, 4))
+    for i in range(4):
+        result = result + fr[i].astype(F32)
     out_ref[...] = result.astype(BF)
     for copy in pending:
         copy.wait_send()
+    for owner, copy in local:
+        pl.when(owner != h)(copy.wait_send)
 
 
 MESSAGES = 8 + 20 + 17 + 4 + 20 + 4
 
 
-def moe(part, hidden, gain, router_t, routes_t, live, win, wout, sin, sout):
+def moe(context, hidden, gain, router_t, routes_t, live, wvu, wo, win, wout, sin, sout):
     vmem = pl.BlockSpec(memory_space=pltpu.VMEM)
     hbm = pl.BlockSpec(memory_space=pl.ANY)
     return pl.pallas_call(
         moe_kernel,
         out_shape=jax.ShapeDtypeStruct((32, 512), BF),
-        in_specs=[vmem] * 6 + [hbm] * 4,
+        in_specs=[vmem] * 6 + [hbm] * 6,
         out_specs=vmem,
         scratch_shapes=[
+            pltpu.VMEM((4, 512, 128), BF),
+            pltpu.VMEM((512, 2048), BF),
+            pltpu.VMEM((4, 32, 512), BF),
             pltpu.VMEM((4, 352, 2048), BF),
             pltpu.VMEM((2, 352, 2048), BF),
             pltpu.VMEM((2, 352, 2048), BF),
@@ -401,7 +474,8 @@
             pltpu.VMEM((4, 32, 512), BF),
             pltpu.VMEM((32, 2048), BF),
             pltpu.VMEM((2, 1024, 1152), BF),
-            pltpu.VMEM((4, 32, 512), F32),
+            pltpu.VMEM((4, 32, 512), BF),
+            pltpu.VMEM((32, 352), F32),
             pltpu.VMEM((2, 256, 2048), BF),
             pltpu.VMEM((256, 352), BF),
             pltpu.VMEM((4, 128, 2048), BF),
@@ -413,15 +487,15 @@
             pltpu.VMEM((4, 2, 64, 1024), BF),
             pltpu.VMEM((2, 32, 1024), BF),
             pltpu.VMEM((2, 64, 1024), BF),
-            pltpu.VMEM((32, 1024), BF),
             pltpu.VMEM((4, 32, 512), BF),
             pltpu.VMEM((3, 32, 512), BF),
-            pltpu.SemaphoreType.DMA((4,)),
+            pltpu.SemaphoreType.DMA((6,)),
             pltpu.SemaphoreType.DMA((MESSAGES,)),
             pltpu.SemaphoreType.DMA((MESSAGES,)),
+            pltpu.SemaphoreType.DMA((8,)),
         ],
         compiler_params=pltpu.CompilerParams(collective_id=1, has_side_effects=True, vmem_limit_bytes=60 << 20),
-    )(part, hidden, gain, router_t, routes_t, live, win, wout, sin, sout)
+    )(context, hidden, gain, router_t, routes_t, live, wvu, wo, win, wout, sin, sout)
 
 
 def body(
@@ -489,21 +563,17 @@
         context
         + prob_new.astype(jnp.float32)[..., None] * key_new[:, None, :LAT].astype(jnp.float32)
     ).astype(jnp.bfloat16)
-    values = jnp.einsum(
-        "rhc,hcv->rhv", context, w_value_up, preferred_element_type=jnp.float32
-    ).astype(jnp.bfloat16)
-    partial_value = jnp.dot(
-        values.reshape(request_count, local_heads * VDIM), w_out, preferred_element_type=jnp.float32
-    ).astype(jnp.bfloat16)
     experts_in = jnp.transpose(w_experts_in, (0, 2, 3, 1)).reshape(4, 352, 2048)
     shared_in = jnp.transpose(w_shared_in, (1, 2, 0))
     return moe(
-        partial_value,
+        jnp.transpose(context, (1, 0, 2)),
         hidden,
         mlp_gain.reshape(1, -1),
         w_router.T,
         routes.T,
         live_mask.reshape(1, -1),
+        w_value_up,
+        w_out,
         experts_in,
         w_experts_out,
         shared_in,

time: 97.7 us -> 95.3 us (0.975)
  matrix products: 13.1 us -> 11.2 us
  Pallas kernels: 77.9 us -> 76.3 us
    dot_general x2 -> x0, matrix products: 4.05 us -> none  [the longest x1 2.7 us: body(): jnp.dot(values.reshape(request_count, local_heads * VDIM), w_out, preferr...]
    dot_general x1, matrix products: 1.21 us -> 3.41 us  [body(): jnp.einsum('rhj,rjc->rhc', probabilities, kv_cache[..., :LAT], preferred_...]
    pallas_call x1, Pallas kernels: 70.5 us -> 68.9 us  [moe(): pl.pallas_call(moe_kernel, out_shape=jax.ShapeDtypeStruct((32, 512), BF),...]
    unnamed x13 -> x7, local copies, waits for them, and re-layouts: 2.13 us -> 2.14 us
where the time goes in v2:
time: 95.3 us; the launch traced here: 94.9 us
  Pallas kernels  76.3 us (80%)
  matrix products  11.2 us (12%)
  local copies, waits for them, and re-layouts  4.2 us (4%)
  other arithmetic  3.01 us (3%)
    pallas_call x1, Pallas kernels, moe(): pl.pallas_call(moe_kernel, out_shape=jax.ShapeDtypeStruct((32, 512), BF),...  68.9 us
    pallas_call x1, Pallas kernels, head_gather(): pl.pallas_call(head_gather_kernel, out_shape=jax.ShapeDtypeStruct((4,) +...  7.44 us
    dot_general x1, matrix products, body(): jnp.einsum('rhj,rjc->rhc', probabilities, kv_cache[..., :LAT], preferred_...  3.41 us
    dot_general x1, matrix products, body(): jnp.einsum('rhc,rjc->rhj', query_full, kv_cache, preferred_element_type=j...  3.2 us
    unnamed x7, local copies, waits for them, and re-layouts  2.14 us

profile of v2, /device:TPU:1, one launch (start us, length us, event | category | flops | bytes accessed | tf_op | source)
XLA Modules:
  0.0 94.9 jit_solution(4110387821854432848)
XLA Ops:
  0.0 0.0 copy-start
  0.0 0.0 copy-start.2
  0.0 1.2 %fusion.4 = f32[32]{0:T(128)S(1)} fusion(bf16[32,2048]{1,0:T(8,128)(2,1)} %hid_ref.1), kind=kLoop, calls=%fused_computation.9 | loop fusion | flops 196576 | bytes 131200 | tf_op jit(solution)/shard_map/reduce_sum | solution.py:28
  1.2 0.8 copy-done
  2.0 1.6 %fusion.17 = f32[32,768]{1,0:T(8,128)S(1)} fusion(bf16[2048,768]{1,0:T(8,128)(2,1)S(1)} %copy-done, bf16[32,2048]{1,0:T(8,128)(2,1)} %hid_ref.1, f32[2048]{0:T(1024)} %param.19, f32[32]{0:T(128)S(1)} %add_rsqrt_fusion.1), kind=kOutput, calls=%fused_computation.31 | convolution fusion | flops 100925440 | bytes 3383424 | tf_op jit(solution)/shard_map/dot_general | solution.py:525
  3.5 0.0 copy-start.1
  3.5 0.1 reshape.121
  3.7 0.1 fusion.27
  3.8 1.5 %convolution_convert_fusion.1 = bf16[32,144]{1,0:T(8,128)(2,1)S(1)} fusion(bf16[2048,144]{0,1:T(8,128)(2,1)} %param.21, bf16[32,2048]{1,0:T(8,128)(2,1)} %hid_ref.1, f32[2048]{0:T(1024)} %param.19, f32[32]{0:T(128)S(1)} %add_rsqrt_fusion.1), kind=kOutput, calls=%fused_computation.6 | convolution fusion | flops 19141120 | bytes 738432 | tf_op jit(solution)/shard_map/dot_general | solution.py:534
  5.3 0.6 pad.4.x_ref
  5.9 7.4 %shard_map.172 = bf16[4,32,256]{2,1,0:T(8,128)(2,1)} custom-call(bf16[32,256]{1,0:T(8,128)(2,1)} %pad.4.x_ref), custom_call_target="tpu_custom_call" | custom-call | tf_op jit(solution)/shard_map/pallas_call | solution.py:81
  13.3 0.8 slice_bitcast_fusion.3
  14.1 0.1 slice_convert_fusion
  14.2 0.0 copy-done.2
  14.2 0.1 subtract_convert_fusion.1
  14.4 1.2 %fusion.2 = bf16[32,4,512]{2,0,1:T(8,128)(2,1)S(1)} fusion(bf16[4,128,512]{2,1,0:T(8,128)(2,1)} %param.23, bf16[32,4,128]{2,1,0:T(4,128)(2,1)S(1)} %slice.56), kind=kOutput, calls=%fused_computation.3 | convolution fusion | flops 16842752 | bytes 688128 | tf_op jit(solution)/shard_map/rhn,hnc->rhc/dot_general | solution.py:531
  15.7 0.1 pad_maximum_fusion
  15.8 0.1 iota_compare_fusion
  15.8 3.2 %fusion.28 = (f32[32,4]{1,0:T(8,128)S(1)}, f32[32,4,128]{2,1,0:T(4,128)S(1)}) fusion(bf16[32,128,576]{1,2,0:T(8,128)(2,1)} %param.26, bf16[32,4,576]{2,0,1:T(8,128)(2,1)S(1)} %pad_maximum_fusion, pred[32,128]{1,0:T(8,128)(4,1)S(1)} %iota_compare_fusion), kind=kOutput, calls=%fused_computation.60 | convolution fusion | flops 18923392 | bytes 4936192 | tf_op jit(solution)/shard_map/rhc,rjc->rhj/dot_general | solution.py:544
  19.0 0.1 copy.38
  19.1 0.2 fusion.12
  19.3 0.0 copy-done.1
  19.3 0.1 fusion.25
  19.4 0.1 maximum_bitcast_fusion
  19.5 0.3 fusion.8
  19.8 0.1 copy.47
  19.9 0.1 copy.39
  20.0 0.2 fusion.15
  20.2 0.1 copy.40
  20.3 0.1 copy.41
  20.4 3.4 %fusion = f32[32,4,512]{2,1,0:T(4,128)S(1)} fusion(bf16[32,128,576]{1,2,0:T(8,128)(2,1)} %param.26, f32[32,4,128]{2,1,0:T(4,128)S(1)} %get-tuple-element.20, f32[32,4]{1,0:T(8,128)S(1)} %copy.41, f32[32,4]{1,0:T(8,128)S(1)} %copy.39), kind=kOutput, calls=%fused_computation | convolution fusion | flops 16826368 | bytes 4523008 | tf_op jit(solution)/shard_map/rhj,rjc->rhc/dot_general | solution.py:559
  23.8 0.8 fusion.7.ctx_ref
  24.6 68.9 %shard_map.173 = bf16[32,512]{1,0:T(8,128)(2,1)} custom-call(bf16[4,32,512]{2,1,0:T(8,128)(2,1)} %fusion.7.ctx_ref, bf16[32,2048]{1,0:T(8,128)(2,1)} %hid_ref.1, f32[1,2048]{1,0:T(1,128)} %bitcast.61, bf16[64,2048]{1,0:T(8,128)(2,1)} %bitcast.60, s32[6,32]{1,0:T(8,128)} %bitcast.62, s32[1,32]{1,0:T(1,128)} %bitcast.63, bf16[4,512,128]{2,1,0:T(8,128)(2,1)} %wvu_hbm.1, ...), custom_call_target="tpu_custom_call" | custom-call | tf_op jit(solution)/shard_map/pallas_call | solution.py:460
  93.5 1.4 %copy.68 = bf16[32,512]{1,0:T(8,128)(2,1)} copy(bf16[32,512]{1,0:T(8,128)(2,1)} %shard_map.173) | data formatting | bytes 65536
  (9 shorter events, 0.1 us)
Async XLA Ops:
  0.0 2.0 %copy-start = (bf16[2048,768]{1,0:T(8,128)(2,1)S(1)}, bf16[2048,768]{1,0:T(8,128)(2,1)}, u32[]{:S(2)}) copy-start(bf16[2048,768]{1,0:T(8,128)(2,1)} %param.20) | copy-start | bytes 9437188
  0.0 14.2 %copy-start.2 = (s32[32]{0:T(128)S(1)}, s32[32]{0:T(128)}, u32[]{:S(2)}) copy-start(s32[32]{0:T(128)} %param.27) | copy-start | bytes 388
  3.5 15.8 %copy-start.1 = (f32[512]{0:T(512)S(1)}, f32[512]{0:T(512)}, u32[]{:S(2)}) copy-start(f32[512]{0:T(512)} %param.22) | copy-start | bytes 6148

commit v3 on v2

--- a/solution.py
+++ b/solution.py
@@ -46,29 +46,33 @@
     )
 
 
-def head_gather_kernel(x_ref, o_ref, ssem, rsem):
+def front_kernel(hid_ref, gain_ref, wlat_ref, wq_hbm, o_ref, q_ref, wq, fresh, wsem, ssem, rsem):
     dp, h = lax.axis_index("dp"), lax.axis_index("head")
+    weight = pltpu.make_async_copy(wq_hbm, wq, wsem)
+    weight.start()
     barrier = pltpu.get_barrier_semaphore()
     for k in range(1, 4):
         pl.semaphore_signal(barrier, inc=1, device_id=(dp, lax.rem(h + k, 4)), device_id_type=MESH)
+    normed = rms_norm(hid_ref[...].astype(F32), gain_ref[...]).astype(BF)
+    width = wlat_ref.shape[0]
+    fresh[...] = jnp.zeros_like(fresh)
+    fresh[:, 0:width] = lax.dot_general(normed, wlat_ref[...], NT, preferred_element_type=F32).astype(BF)
     pl.semaphore_wait(barrier, 3)
-    copies = []
-    for k in range(1, 4):
-        copies.append(
-            pltpu.make_async_remote_copy(
-                src_ref=x_ref,
-                dst_ref=o_ref.at[h],
-                send_sem=ssem.at[k - 1],
-                recv_sem=rsem.at[k - 1],
-                device_id=(dp, lax.rem(h + k, 4)),
-                device_id_type=MESH,
-            )
-        )
-        copies[-1].start()
-    o_ref[h] = x_ref[...]
     for k in range(1, 4):
         pltpu.make_async_remote_copy(
-            src_ref=x_ref,
+            src_ref=fresh,
+            dst_ref=o_ref.at[h],
+            send_sem=ssem.at[k - 1],
+            recv_sem=rsem.at[k - 1],
+            device_id=(dp, lax.rem(h + k, 4)),
+            device_id_type=MESH,
+        ).start()
+    o_ref[h] = fresh[...]
+    weight.wait()
+    q_ref[...] = jnp.dot(normed, wq[...], preferred_element_type=F32)
+    for k in range(1, 4):
+        pltpu.make_async_remote_copy(
+            src_ref=fresh,
             dst_ref=o_ref.at[lax.rem(h + 4 - k, 4)],
             send_sem=ssem.at[k - 1],
             recv_sem=rsem.at[k - 1],
@@ -77,21 +81,32 @@
         ).wait()
 
 
-def head_gather(x):
+def front(hidden, gain, w_latent_t, w_query):
+    vmem = pl.BlockSpec(memory_space=pltpu.VMEM)
+    rows = hidden.shape[0]
     return pl.pallas_call(
-        head_gather_kernel,
-        out_shape=jax.ShapeDtypeStruct((4,) + x.shape, x.dtype),
-        in_specs=[pl.BlockSpec(memory_space=pltpu.VMEM)],
-        out_specs=pl.BlockSpec(memory_space=pltpu.VMEM),
-        scratch_shapes=[pltpu.SemaphoreType.DMA((3,)), pltpu.SemaphoreType.DMA((3,))],
-        compiler_params=pltpu.CompilerParams(collective_id=0, has_side_effects=True),
-    )(x)
+        front_kernel,
+        out_shape=(
+            jax.ShapeDtypeStruct((4, rows, 256), BF),
+            jax.ShapeDtypeStruct((rows, w_query.shape[1]), F32),
+        ),
+        in_specs=[vmem, vmem, vmem, pl.BlockSpec(memory_space=pl.ANY)],
+        out_specs=(vmem, vmem),
+        scratch_shapes=[
+            pltpu.VMEM(w_query.shape, BF),
+            pltpu.VMEM((rows, 256), BF),
+            pltpu.SemaphoreType.DMA,
+            pltpu.SemaphoreType.DMA((3,)),
+            pltpu.SemaphoreType.DMA((3,)),
+        ],
+        compiler_params=pltpu.CompilerParams(collective_id=0, has_side_effects=True, vmem_limit_bytes=24 << 20),
+    )(hidden, gain, w_latent_t, w_query)
 
 
 def moe_kernel(
-    ctx_ref, hid_ref, gain_ref, rt_ref, routes_ref, live_ref, wvu_hbm, wo_hbm, win_hbm, wout_hbm, sin_hbm, sout_hbm,
+    val_ref, hid_ref, gain_ref, rt_ref, routes_ref, live_ref, wo_hbm, win_hbm, wout_hbm, sin_hbm, sout_hbm,
     out_ref,
-    wvu, wo, part, win, wout, sin, sout, yrs, mix, ffn, xb, shared, gate_s, xs, hid_slot, outs, pmat, wslot, cb, pr, rl, rf,
+    wo, part, win, wout, sin, sout, yrs, mix, ffn, xb, shared, gate_s, xs, hid_slot, outs, pmat, wslot, cb, pr, rl, rf,
     al, af, fr, yr,
     wsem, ssem, rsem, fsem,
 ):
@@ -126,8 +141,8 @@
             )
         )
     ]
-    first_weights = [pltpu.make_async_copy(wvu_hbm, wvu, wsem.at[4]), pltpu.make_async_copy(wo_hbm, wo, wsem.at[5])]
-    for copy in first_weights + weights:
+    out_weight = pltpu.make_async_copy(wo_hbm, wo, wsem.at[4])
+    for copy in [out_weight] + weights:
         copy.start()
 
     barrier = pltpu.get_barrier_semaphore()
@@ -135,13 +150,9 @@
     diagonal = tuple((other_dp, lax.rem(h + k, 4)) for k in range(1, 4))
     for peer in (ypeer(1), ypeer(2), ypeer(3), dev(1, 0), dev(-1, 0), dev(0, 1), dev(0, -1), partner) + diagonal:
         pl.semaphore_signal(barrier, inc=1, device_id=peer, device_id_type=MESH)
-    first_weights[0].wait()
-    values = jnp.concatenate(
-        [jnp.dot(ctx_ref[i], wvu[i], preferred_element_type=F32).astype(BF) for i in range(4)], axis=1
-    )
-    first_weights[1].wait()
+    out_weight.wait()
     for i in range(4):
-        part[i] = jnp.dot(values, wo[:, i * 512 : (i + 1) * 512], preferred_element_type=F32).astype(BF)
+        part[i] = jnp.dot(val_ref[...], wo[:, i * 512 : (i + 1) * 512], preferred_element_type=F32).astype(BF)
     pl.semaphore_wait(barrier, 11)
 
     pending = []
@@ -454,16 +465,15 @@
 MESSAGES = 8 + 20 + 17 + 4 + 20 + 4
 
 
-def moe(context, hidden, gain, router_t, routes_t, live, wvu, wo, win, wout, sin, sout):
+def moe(values, hidden, gain, router_t, routes_t, live, wo, win, wout, sin, sout):
     vmem = pl.BlockSpec(memory_space=pltpu.VMEM)
     hbm = pl.BlockSpec(memory_space=pl.ANY)
     return pl.pallas_call(
         moe_kernel,
         out_shape=jax.ShapeDtypeStruct((32, 512), BF),
-        in_specs=[vmem] * 6 + [hbm] * 6,
+        in_specs=[vmem] * 6 + [hbm] * 5,
         out_specs=vmem,
         scratch_shapes=[
-            pltpu.VMEM((4, 512, 128), BF),
             pltpu.VMEM((512, 2048), BF),
             pltpu.VMEM((4, 32, 512), BF),
             pltpu.VMEM((4, 352, 2048), BF),
@@ -489,13 +499,13 @@
             pltpu.VMEM((2, 64, 1024), BF),
             pltpu.VMEM((4, 32, 512), BF),
             pltpu.VMEM((3, 32, 512), BF),
-            pltpu.SemaphoreType.DMA((6,)),
+            pltpu.SemaphoreType.DMA((5,)),
             pltpu.SemaphoreType.DMA((MESSAGES,)),
             pltpu.SemaphoreType.DMA((MESSAGES,)),
             pltpu.SemaphoreType.DMA((8,)),
         ],
         compiler_params=pltpu.CompilerParams(collective_id=1, has_side_effects=True, vmem_limit_bytes=60 << 20),
-    )(context, hidden, gain, router_t, routes_t, live, wvu, wo, win, wout, sin, sout)
+    )(values, hidden, gain, router_t, routes_t, live, wo, win, wout, sin, sout)
 
 
 def body(
@@ -521,19 +531,15 @@
     request_count = hidden.shape[0]
     local_heads = w_key_up.shape[0]
     cache_length = kv_cache.shape[1]
-    normed = rms_norm(hidden.astype(jnp.float32), attn_gain).astype(jnp.bfloat16)
-    query_all = jnp.dot(normed, w_query, preferred_element_type=jnp.float32).reshape(
-        request_count, local_heads, NOPE + ROPE
-    )
+    gathered, query_all = front(hidden, attn_gain.reshape(1, -1), w_latent.T, w_query)
+    query_all = query_all.reshape(request_count, local_heads, NOPE + ROPE)
     positions = lengths.astype(jnp.float32)
     query_nope = query_all[..., :NOPE].astype(jnp.bfloat16)
     query_rope = rotary(query_all[..., NOPE:], positions).astype(jnp.bfloat16)
     query_latent = jnp.einsum(
         "rhn,hnc->rhc", query_nope, w_key_up, preferred_element_type=jnp.float32
     ).astype(jnp.bfloat16)
-    fresh_part = jnp.dot(normed, w_latent, preferred_element_type=jnp.float32).astype(jnp.bfloat16)
-    width = fresh_part.shape[1]
-    gathered = head_gather(jnp.pad(fresh_part, ((0, 0), (0, 256 - width))))
+    width = w_latent.shape[1]
     fresh_kv = jnp.concatenate([gathered[i, :, :width] for i in range(4)], axis=1)
     latent_new = rms_norm(fresh_kv[:, :LAT].astype(jnp.float32), latent_gain)
     rope_new = rotary(fresh_kv[:, LAT:].astype(jnp.float32), positions)
@@ -563,16 +569,18 @@
         context
         + prob_new.astype(jnp.float32)[..., None] * key_new[:, None, :LAT].astype(jnp.float32)
     ).astype(jnp.bfloat16)
+    values = jnp.einsum(
+        "rhc,hcv->rhv", context, w_value_up, preferred_element_type=jnp.float32
+    ).astype(jnp.bfloat16)
     experts_in = jnp.transpose(w_experts_in, (0, 2, 3, 1)).reshape(4, 352, 2048)
     shared_in = jnp.transpose(w_shared_in, (1, 2, 0))
     return moe(
-        jnp.transpose(context, (1, 0, 2)),
+        values.reshape(request_count, local_heads * VDIM),
         hidden,
         mlp_gain.reshape(1, -1),
         w_router.T,
         routes.T,
         live_mask.reshape(1, -1),
-        w_value_up,
         w_out,
         experts_in,
         w_experts_out,

time: 95.3 us -> 89.5 us (0.939)
  matrix products: 11.2 us -> 5.28 us
  local copies, waits for them, and re-layouts: 4.2 us -> 6.95 us
  Pallas kernels: 76.3 us -> 75 us
  other arithmetic: 3.01 us -> 1.84 us
    unnamed x7 -> x19, local copies, waits for them, and re-layouts: 2.14 us -> 6 us
    dot_general x2 -> x1, matrix products: 3.07 us -> 0.31 us  [body(): jnp.einsum('rhc,hcv->rhv', context, w_value_up, preferred_element_type=jn...]
    dot_general x1, matrix products: 3.41 us -> 1.21 us  [body(): jnp.einsum('rhj,rjc->rhc', probabilities, kv_cache[..., :LAT], preferred_...]
    reduce_sum x2 -> x1, other arithmetic: 1.39 us -> 0.2 us  [rms_norm(): mean_square = jnp.mean(values * values, axis=-1, keepdims=True)]
    pallas_call x1, Pallas kernels: 7.44 us -> 6.34 us  [front(): pl.pallas_call(front_kernel, out_shape=(jax.ShapeDtypeStruct((4, rows, 25...]
    dot_general x1, matrix products: 1.23 us -> 0.19 us  [body(): jnp.einsum('rhn,hnc->rhc', query_nope, w_key_up, preferred_element_type=j...]
where the time goes in v3:
time: 89.5 us; the launch traced here: 89.2 us
  Pallas kernels  75 us (84%)
  local copies, waits for them, and re-layouts  6.95 us (8%)
  matrix products  5.28 us (6%)
  other arithmetic  1.84 us (2%)
    pallas_call x1, Pallas kernels, moe(): pl.pallas_call(moe_kernel, out_shape=jax.ShapeDtypeStruct((32, 512), BF),...  68.7 us
    pallas_call x1, Pallas kernels, front(): pl.pallas_call(front_kernel, out_shape=(jax.ShapeDtypeStruct((4, rows, 25...  6.34 us
    unnamed x19, local copies, waits for them, and re-layouts  6 us
    dot_general x1, matrix products, body(): jnp.einsum('rhc,rjc->rhj', query_full, kv_cache, preferred_element_type=j...  3.28 us

profile of v3, /device:TPU:1, one launch (start us, length us, event | category | flops | bytes accessed | tf_op | source)
XLA Modules:
  0.0 89.2 jit_solution(8985632686655851450)
XLA Ops:
  0.0 0.0 copy-start
  0.0 0.0 copy-start.8
  0.0 0.0 copy-start.1
  0.0 1.9 %copy-done.1 = bf16[2048,768]{1,0:T(8,128)(2,1)S(1)} copy-done((bf16[2048,768]{1,0:T(8,128)(2,1)S(1)}, bf16[2048,768]{1,0:T(8,128)(2,1)}, u32[]{:S(2)}) %copy-start.1) | copy-done | bytes 3145752
  2.0 0.0 copy-start.2
  2.0 1.1 %copy-done.2 = bf16[2048,144]{0,1:T(8,128)(2,1)S(1)} copy-done((bf16[2048,144]{0,1:T(8,128)(2,1)S(1)}, bf16[2048,144]{0,1:T(8,128)(2,1)}, u32[]{:S(2)}) %copy-start.2) | copy-done | bytes 589848
  3.0 0.0 copy-start.3
  3.0 0.9 %copy-done.3 = bf16[32,2048]{1,0:T(8,128)(2,1)S(1)} copy-done((bf16[32,2048]{1,0:T(8,128)(2,1)S(1)}, bf16[32,2048]{1,0:T(8,128)(2,1)}, u32[]{:S(2)}) %copy-start.3) | copy-done | bytes 131096
  3.9 0.0 copy-start.4
  3.9 0.7 copy-done.4
  4.6 0.0 copy-start.7
  4.6 6.3 %shard_map.172 = (bf16[4,32,256]{2,1,0:T(8,128)(2,1)S(1)}, f32[32,768]{1,0:T(8,128)S(1)}) custom-call(bf16[32,2048]{1,0:T(8,128)(2,1)S(1)} %copy-done.3, f32[1,2048]{1,0:T(1,128)S(1)} %bitcast.34, bf16[144,2048]{1,0:T(8,128)(2,1)S(1)} %bitcast.33, bf16[2048,768]{1,0:T(8,128)(2,1)S(1)} %copy-done.1), custom_call_target="tpu_custom_call" | custom-call | tf_op jit(solution)/shard_map/pallas_call | solution.py:87
  11.0 0.1 reshape.119
  11.1 0.0 copy-start.5
  11.1 0.1 fusion.23
  11.2 0.1 slice_convert_fusion
  11.3 0.8 convert_element_type.42
  12.1 0.1 subtract_convert_fusion.1
  12.3 0.0 copy-done
  12.3 0.2 fusion.2
  12.5 0.1 pad_maximum_fusion
  12.6 0.0 copy-done.8
  12.6 0.1 iota_compare_fusion
  12.7 0.0 copy-start.6
  12.7 3.3 %fusion.24 = (f32[32,4]{1,0:T(8,128)S(1)}, f32[32,4,128]{2,1,0:T(4,128)S(1)}) fusion(bf16[32,128,576]{1,2,0:T(8,128)(2,1)} %param.26, bf16[32,4,576]{2,0,1:T(8,128)(2,1)S(1)} %pad_maximum_fusion, pred[32,128]{1,0:T(8,128)(4,1)S(1)} %iota_compare_fusion), kind=kOutput, calls=%fused_computation.54 | convolution fusion | flops 18923392 | bytes 4936192 | tf_op jit(solution)/shard_map/rhc,rjc->rhj/dot_general | solution.py:550
  16.0 0.2 fusion.13
  16.2 0.0 copy-done.7
  16.2 0.1 fusion.21
  16.3 0.1 maximum_bitcast_fusion
  16.4 0.3 fusion.9
  16.7 0.2 fusion.16
  16.9 0.0 copy-done.5
  16.9 1.2 %fusion = f32[32,4,512]{2,1,0:T(4,128)S(1)} fusion(bf16[32,128,576]{1,2,0:T(8,128)(2,1)S(1)} %copy-done.5, f32[32,4,128]{2,1,0:T(4,128)S(1)} %get-tuple-element.26, f32[32,4]{1,0:T(8,128)S(1)} %get-tuple-element.20, f32[32,4]{1,0:T(8,128)S(1)} %multiply_maximum_fusion), kind=kOutput, calls=%fused_computation | convolution fusion | flops 16826368 | bytes 4554752 | tf_op jit(solution)/shard_map/rhj,rjc->rhc/dot_general | solution.py:565
  18.2 0.1 copy.23
  18.2 0.0 copy-done.6
  18.2 0.3 fusion.4
  18.6 0.6 copy.51
  19.2 68.7 %shard_map.173 = bf16[32,512]{1,0:T(8,128)(2,1)} custom-call(bf16[32,512]{1,0:T(8,128)(2,1)} %bitcast.38, bf16[32,2048]{1,0:T(8,128)(2,1)} %hid_ref.3, f32[1,2048]{1,0:T(1,128)} %bitcast.41, bf16[64,2048]{1,0:T(8,128)(2,1)} %bitcast.37, s32[6,32]{1,0:T(8,128)} %bitcast.42, s32[1,32]{1,0:T(1,128)} %bitcast.43, bf16[512,2048]{1,0:T(8,128)(2,1)} %wo_hbm.1, ...), custom_call_target="tpu_custom_call" | custom-call | tf_op jit(solution)/shard_map/pallas_call | solution.py:471
  87.8 1.4 %copy.53 = bf16[32,512]{1,0:T(8,128)(2,1)} copy(bf16[32,512]{1,0:T(8,128)(2,1)} %shard_map.173) | data formatting | bytes 65536
  (7 shorter events, 0.1 us)
Async XLA Ops:
  0.0 12.3 %copy-start = (bf16[4,128,512]{2,1,0:T(8,128)(2,1)S(1)}, bf16[4,128,512]{2,1,0:T(8,128)(2,1)}, u32[]{:S(2)}) copy-start(bf16[4,128,512]{2,1,0:T(8,128)(2,1)} %param.23) | copy-start | bytes 1572868
  0.0 12.6 %copy-start.8 = (s32[32]{0:T(128)S(1)}, s32[32]{0:T(128)}, u32[]{:S(2)}) copy-start(s32[32]{0:T(128)} %param.27) | copy-start | bytes 388
  0.0 1.9 %copy-start.1 = (bf16[2048,768]{1,0:T(8,128)(2,1)S(1)}, bf16[2048,768]{1,0:T(8,128)(2,1)}, u32[]{:S(2)}) copy-start(bf16[2048,768]{1,0:T(8,128)(2,1)} %wq_hbm.1) | copy-start | bytes 9437188
  2.0 1.1 %copy-start.2 = (bf16[2048,144]{0,1:T(8,128)(2,1)S(1)}, bf16[2048,144]{0,1:T(8,128)(2,1)}, u32[]{:S(2)}) copy-start(bf16[2048,144]{0,1:T(8,128)(2,1)} %param.21) | copy-start | bytes 1769476
  3.0 0.9 %copy-start.3 = (bf16[32,2048]{1,0:T(8,128)(2,1)S(1)}, bf16[32,2048]{1,0:T(8,128)(2,1)}, u32[]{:S(2)}) copy-start(bf16[32,2048]{1,0:T(8,128)(2,1)} %hid_ref.3) | copy-start | bytes 393220
  3.9 0.7 copy-start.4
  4.6 11.6 %copy-start.7 = (f32[512]{0:T(512)S(1)}, f32[512]{0:T(512)}, u32[]{:S(2)}) copy-start(f32[512]{0:T(512)} %param.22) | copy-start | bytes 6148
  11.1 5.8 %copy-start.5 = (bf16[32,128,576]{1,2,0:T(8,128)(2,1)S(1)}, bf16[32,128,576]{1,2,0:T(8,128)(2,1)}, u32[]{:S(2)}) copy-start(bf16[32,128,576]{1,2,0:T(8,128)(2,1)} %param.26) | copy-start | bytes 14155780
  12.7 5.5 %copy-start.6 = (bf16[4,512,128]{2,1,0:T(8,128)(2,1)S(1)}, bf16[4,512,128]{2,1,0:T(8,128)(2,1)}, u32[]{:S(2)}) copy-start(bf16[4,512,128]{2,1,0:T(8,128)(2,1)} %param.24) | copy-start | bytes 1572868

commit v4 on v3

--- a/solution.py
+++ b/solution.py
@@ -46,17 +46,22 @@
     )
 
 
-def front_kernel(hid_ref, gain_ref, wlat_ref, wq_hbm, o_ref, q_ref, wq, fresh, wsem, ssem, rsem):
+def front_kernel(gain_ref, hid_hbm, wlat_hbm, wq_hbm, o_ref, q_ref, hid, wlat, wq, fresh, wsem, ssem, rsem):
     dp, h = lax.axis_index("dp"), lax.axis_index("head")
-    weight = pltpu.make_async_copy(wq_hbm, wq, wsem)
-    weight.start()
+    loads = [
+        pltpu.make_async_copy(s, d, wsem.at[i]) for i, (s, d) in enumerate(((hid_hbm, hid), (wlat_hbm, wlat), (wq_hbm, wq)))
+    ]
+    for copy in loads:
+        copy.start()
     barrier = pltpu.get_barrier_semaphore()
     for k in range(1, 4):
         pl.semaphore_signal(barrier, inc=1, device_id=(dp, lax.rem(h + k, 4)), device_id_type=MESH)
-    normed = rms_norm(hid_ref[...].astype(F32), gain_ref[...]).astype(BF)
-    width = wlat_ref.shape[0]
     fresh[...] = jnp.zeros_like(fresh)
-    fresh[:, 0:width] = lax.dot_general(normed, wlat_ref[...], NT, preferred_element_type=F32).astype(BF)
+    loads[0].wait()
+    normed = rms_norm(hid[...].astype(F32), gain_ref[...]).astype(BF)
+    width = wlat.shape[0]
+    loads[1].wait()
+    fresh[:, 0:width] = lax.dot_general(normed, wlat[...], NT, preferred_element_type=F32).astype(BF)
     pl.semaphore_wait(barrier, 3)
     for k in range(1, 4):
         pltpu.make_async_remote_copy(
@@ -68,7 +73,7 @@
             device_id_type=MESH,
         ).start()
     o_ref[h] = fresh[...]
-    weight.wait()
+    loads[2].wait()
     q_ref[...] = jnp.dot(normed, wq[...], preferred_element_type=F32)
     for k in range(1, 4):
         pltpu.make_async_remote_copy(
@@ -90,17 +95,19 @@
             jax.ShapeDtypeStruct((4, rows, 256), BF),
             jax.ShapeDtypeStruct((rows, w_query.shape[1]), F32),
         ),
-        in_specs=[vmem, vmem, vmem, pl.BlockSpec(memory_space=pl.ANY)],
+        in_specs=[vmem] + [pl.BlockSpec(memory_space=pltpu.HBM)] * 3,
         out_specs=(vmem, vmem),
         scratch_shapes=[
+            pltpu.VMEM(hidden.shape, BF),
+            pltpu.VMEM(w_latent_t.shape, BF),
             pltpu.VMEM(w_query.shape, BF),
             pltpu.VMEM((rows, 256), BF),
-            pltpu.SemaphoreType.DMA,
+            pltpu.SemaphoreType.DMA((3,)),
             pltpu.SemaphoreType.DMA((3,)),
             pltpu.SemaphoreType.DMA((3,)),
         ],
-        compiler_params=pltpu.CompilerParams(collective_id=0, has_side_effects=True, vmem_limit_bytes=24 << 20),
-    )(hidden, gain, w_latent_t, w_query)
+        compiler_params=pltpu.CompilerParams(collective_id=0, has_side_effects=True, vmem_limit_bytes=67043328),
+    )(gain, hidden, w_latent_t, w_query)
 
 
 def moe_kernel(

time: 89.5 us -> 89.7 us (level)
  local copies, waits for them, and re-layouts: 6.95 us -> 4.14 us
  Pallas kernels: 75 us -> 76.2 us
  matrix products: 5.28 us -> 6.32 us
    unnamed x19 -> x7, local copies, waits for them, and re-layouts: 6 us -> 1.39 us
    pallas_call x1, Pallas kernels: 6.34 us -> 8.04 us  [front(): pl.pallas_call(front_kernel, out_shape=(jax.ShapeDtypeStruct((4, rows, 25...]
    dot_general x1, matrix products: 0.19 us -> 1.23 us  [body(): jnp.einsum('rhn,hnc->rhc', query_nope, w_key_up, preferred_element_type=j...]
    squeeze x1, local copies, waits for them, and re-layouts: 0.01 us -> 0.93 us  [body(): gathered[i, :, :width]]
where the time goes in v4:
time: 89.7 us; the launch traced here: 89.4 us
  Pallas kernels  76.2 us (85%)
  matrix products  6.32 us (7%)
  local copies, waits for them, and re-layouts  4.14 us (5%)
  other arithmetic  2.64 us (3%)
    pallas_call x1, Pallas kernels, moe(): pl.pallas_call(moe_kernel, out_shape=jax.ShapeDtypeStruct((32, 512), BF),...  68.1 us
    pallas_call x1, Pallas kernels, front(): pl.pallas_call(front_kernel, out_shape=(jax.ShapeDtypeStruct((4, rows, 25...  8.04 us
    dot_general x1, matrix products, body(): jnp.einsum('rhc,rjc->rhj', query_full, kv_cache, preferred_element_type=j...  3.28 us

profile of v4, /device:TPU:1, one launch (start us, length us, event | category | flops | bytes accessed | tf_op | source)
XLA Modules:
  0.0 89.4 jit_solution(7800195906673198230)
XLA Ops:
  0.0 8.0 %shard_map.172 = (bf16[4,32,256]{2,1,0:T(8,128)(2,1)}, f32[32,768]{1,0:T(8,128)}) custom-call(f32[1,2048]{1,0:T(1,128)} %bitcast.40, bf16[32,2048]{1,0:T(8,128)(2,1)} %hid_ref.1, bf16[144,2048]{1,0:T(8,128)(2,1)} %bitcast.35, bf16[2048,768]{1,0:T(8,128)(2,1)} %wq_hbm.1), custom_call_target="tpu_custom_call" | custom-call | tf_op jit(solution)/shard_map/pallas_call | solution.py:92
  8.0 0.0 copy-start.2
  8.1 1.0 %reshape.119 = f32[32,4,192]{2,1,0:T(4,128)S(1)} reshape(f32[32,768]{1,0:T(8,128)} %get-tuple-element.7) | data formatting | bytes 196608 | tf_op jit(solution)/shard_map/reshape | solution.py:542
  9.1 0.0 copy-start
  9.1 0.1 fusion.23
  9.2 0.9 %slice_bitcast_fusion.3 = (bf16[32,144]{1,0:T(8,128)(2,1)S(1)}, bf16[32,144]{1,0:T(8,128)(2,1)S(1)}, bf16[32,144]{1,0:T(8,128)(2,1)S(1)}, bf16[32,144]{1,0:T(8,128)(2,1)S(1)}) fusion(bf16[4,32,256]{2,1,0:T(8,128)(2,1)} %get-tuple-element.8), kind=kLoop, calls=%fused_computation.44 | loop fusion | bytes 73728 | tf_op jit(solution)/shard_map/squeeze | solution.py:550
  10.1 0.1 slice_convert_fusion
  10.2 1.0 %convert_element_type.42 = f32[32]{0:T(128)S(1)} convert(s32[32]{0:T(128)} %param.27) | non-fusion elementwise | flops 32 | bytes 256 | tf_op jit(solution)/shard_map/convert_element_type | solution.py:543
  11.2 0.1 subtract_convert_fusion.1
  11.4 1.2 %fusion.2 = bf16[32,4,512]{2,0,1:T(8,128)(2,1)S(1)} fusion(bf16[4,128,512]{2,1,0:T(8,128)(2,1)} %param.23, bf16[32,4,128]{2,1,0:T(4,128)(2,1)S(1)} %slice.56), kind=kOutput, calls=%fused_computation.3 | convolution fusion | flops 16842752 | bytes 688128 | tf_op jit(solution)/shard_map/rhn,hnc->rhc/dot_general | solution.py:546
  12.6 0.1 pad_maximum_fusion
  12.7 0.7 iota_compare_fusion
  13.4 0.0 copy-start.1
  13.4 3.3 %fusion.24 = (f32[32,4]{1,0:T(8,128)S(1)}, f32[32,4,128]{2,1,0:T(4,128)S(1)}) fusion(bf16[32,128,576]{1,2,0:T(8,128)(2,1)} %param.26, bf16[32,4,576]{2,0,1:T(8,128)(2,1)S(1)} %pad_maximum_fusion, pred[32,128]{1,0:T(8,128)(4,1)S(1)} %iota_compare_fusion), kind=kOutput, calls=%fused_computation.54 | convolution fusion | flops 18923392 | bytes 4936192 | tf_op jit(solution)/shard_map/rhc,rjc->rhj/dot_general | solution.py:557
  16.7 0.2 fusion.13
  16.9 0.0 copy-done.2
  16.9 0.1 fusion.21
  17.0 0.1 maximum_bitcast_fusion
  17.1 0.3 fusion.9
  17.4 0.2 fusion.16
  17.7 0.0 copy-done
  17.7 1.2 %fusion = f32[32,4,512]{2,1,0:T(4,128)S(1)} fusion(bf16[32,128,576]{1,2,0:T(8,128)(2,1)S(1)} %copy-done, f32[32,4,128]{2,1,0:T(4,128)S(1)} %get-tuple-element.26, f32[32,4]{1,0:T(8,128)S(1)} %get-tuple-element.20, f32[32,4]{1,0:T(8,128)S(1)} %multiply_maximum_fusion), kind=kOutput, calls=%fused_computation | convolution fusion | flops 16826368 | bytes 4554752 | tf_op jit(solution)/shard_map/rhj,rjc->rhc/dot_general | solution.py:572
  18.9 0.1 copy.23
  19.0 0.0 copy-done.1
  19.0 0.3 fusion.4
  19.3 0.6 copy.51
  19.9 68.1 %shard_map.173 = bf16[32,512]{1,0:T(8,128)(2,1)} custom-call(bf16[32,512]{1,0:T(8,128)(2,1)} %bitcast.37, bf16[32,2048]{1,0:T(8,128)(2,1)} %hid_ref.1, f32[1,2048]{1,0:T(1,128)} %bitcast.41, bf16[64,2048]{1,0:T(8,128)(2,1)} %bitcast.36, s32[6,32]{1,0:T(8,128)} %bitcast.42, s32[1,32]{1,0:T(1,128)} %bitcast.43, bf16[512,2048]{1,0:T(8,128)(2,1)} %wo_hbm.1, ...), custom_call_target="tpu_custom_call" | custom-call | tf_op jit(solution)/shard_map/pallas_call | solution.py:478
  88.0 1.4 %copy.53 = bf16[32,512]{1,0:T(8,128)(2,1)} copy(bf16[32,512]{1,0:T(8,128)(2,1)} %shard_map.173) | data formatting | bytes 65536
  (6 shorter events, 0.1 us)
Async XLA Ops:
  8.0 8.9 %copy-start.2 = (f32[512]{0:T(512)S(1)}, f32[512]{0:T(512)}, u32[]{:S(2)}) copy-start(f32[512]{0:T(512)} %param.22) | copy-start | bytes 6148
  9.1 8.6 %copy-start = (bf16[32,128,576]{1,2,0:T(8,128)(2,1)S(1)}, bf16[32,128,576]{1,2,0:T(8,128)(2,1)}, u32[]{:S(2)}) copy-start(bf16[32,128,576]{1,2,0:T(8,128)(2,1)} %param.26) | copy-start | bytes 14155780
  13.4 5.5 %copy-start.1 = (bf16[4,512,128]{2,1,0:T(8,128)(2,1)S(1)}, bf16[4,512,128]{2,1,0:T(8,128)(2,1)}, u32[]{:S(2)}) copy-start(bf16[4,512,128]{2,1,0:T(8,128)(2,1)} %param.24) | copy-start | bytes 1572868
